TPU v7x, 768 devices: a whole 4x8x12 slice. The times are simulated.
768 devices in a mesh: gx: 16 (over x_hi, y), gy: 24 (over z, core), gz: 2 (over x_lo).
Axes of the slice: x: 4 (x_hi: 2, x_lo: 2; x = x_hi * 2 + x_lo), y: 8, z: 12, core: 2. Of those that a mesh axis runs over, the one named last changes fastest.
Arguments:
- u_now: float32 [3, 256, 384, 256], P(None, 'gx', 'gy', 'gz'), may hold values from -6 to 6
- u_prev: float32 [3, 256, 384, 256], P(None, 'gx', 'gy', 'gz'), may hold values from -6 to 6
- panels: bfloat16 [16, 2, 384, 48, 256], P('gx', 'gz', 'gy'), may hold values from -6 to 6
- panel_owner: int32 [16, 2, 384, 1], P('gx', 'gz'), may hold values from 0 to 23; in each aligned block of 16 rows (0 to 15, 16 to 31, ..., all dimensions but the last counted through in order) at most 2 rows name the same one
- panel_block: int32 [16, 2, 384], P('gx', 'gz'), may hold values from 0 to 2047
- coupling: float32 [3, 16, 16], replicated, may hold values from -1.5 to 1.5
- layer_depth: int32 [256], P('gz'), may hold values from 0 to 7, never falling along the last dimension, each value on 1 to 64 neighbouring positions
- layer_speed: float32 [8], replicated, may hold values from 0.04 to 0.3
- lateral: float32 [256, 384, 256], P('gx', 'gy', 'gz'), may hold values from 0.5 to 1
Outputs:
- u_final: float32 [3, 256, 384, 256], P(None, 'gx', 'gy', 'gz')
- u_before: float32 [3, 256, 384, 256], P(None, 'gx', 'gy', 'gz')
Inputs may be any that keep to these rules, and one draw needn't show every extreme that they name: `panel_owner`: among the 16 panels of one device (an aligned block of rows) at most 2 have the same owner; in each draw some owner receives exactly 2 from some device. `layer_depth`: layers never decrease with depth; each layer spans 1 to 64 depths.
All inputs are finite; a program needn't handle non-finite values.
Results may differ from a plain program's by a relative error of at most 0.00038.
Values may be sent and summed in bfloat16 or wider, within the bound.
A program may use at most 64 MiB of HBM per device.

v0:
```python
import jax
import jax.numpy as jnp
from jax import lax
from jax.sharding import PartitionSpec as P

NSTEP = 4


def extended(shard, sides, width):
    for axis, dim in sides:
        peers, length = (lax.axis_size(axis), shard.shape[dim])
        up = [(i, (i + 1) % peers) for i in range(peers - 1)]
        down = [(j, i) for i, j in up]
        last = lax.slice_in_dim(shard, length - width, length, axis=dim)
        leading = lax.slice_in_dim(shard, 0, width, axis=dim)
        before = lax.ppermute(last, axis, up)
        after = lax.ppermute(leading, axis, down)
        shard = jnp.concatenate([before, shard, after], axis=dim)
    return shard


def wave_table(count):
    half = count // 2
    freq = 2.0 * jnp.pi * (jnp.arange(half, dtype=jnp.float32) + 0.5) / count
    times = 37.0 + jnp.arange(NSTEP, dtype=jnp.float32)
    phase = freq[:, None] * times[None, :]
    table = jnp.concatenate([jnp.cos(phase), jnp.sin(phase)], axis=0) / jnp.sqrt(jnp.float32(half))
    return table.astype(jnp.bfloat16)


def neighbours(padded, center):
    beside = padded[:, 2:, 1:-1, 1:-1] + padded[:, :-2, 1:-1, 1:-1]
    beside = beside + padded[:, 1:-1, 2:, 1:-1] + padded[:, 1:-1, :-2, 1:-1]
    beside = beside + padded[:, 1:-1, 1:-1, 2:] + padded[:, 1:-1, 1:-1, :-2]
    return beside - 6.0 * center


def per_device(
    u_now, u_prev, panels, panel_owner, panel_block, coupling, layer_depth, layer_speed, lateral
):
    width_gy = lax.axis_size("gy")
    mine = lax.axis_index("gy")
    per_dev = panels.shape[2]
    block_len = coupling.shape[1]
    spectral = panels.shape[4]
    capacity = max(2, 2 * per_dev // width_gy)
    comps, size_x, size_y, size_z = u_now.shape
    zblocks = size_z // block_len
    nblocks = size_x * size_y * zblocks
    table = wave_table(spectral)
    owners = panel_owner.reshape(width_gy, per_dev)
    blocks = panel_block.reshape(width_gy, per_dev)
    target = jnp.arange(width_gy, dtype=jnp.int32)
    hits = (owners[:, :, None] == target[None, None, :]).astype(jnp.int32)
    earlier = jnp.cumsum(hits, axis=1) - hits
    ranks = jnp.sum(earlier * hits, axis=2)
    slot_ids = jnp.arange(capacity, dtype=jnp.int32)
    my_owner = lax.dynamic_index_in_dim(owners, mine, 0, keepdims=False)
    my_rank = lax.dynamic_index_in_dim(ranks, mine, 0, keepdims=False)
    send_pick = (my_owner[None, None, :] == target[:, None, None]) & (
        my_rank[None, None, :] == slot_ids[None, :, None]
    )
    send_pick = send_pick.reshape(width_gy * capacity, per_dev)
    recv_pick = (
        (owners[:, None, :] == mine) & (ranks[:, None, :] == slot_ids[None, :, None])
    ).astype(jnp.int32)
    slot_block = jnp.sum(recv_pick * blocks[:, None, :], axis=2).reshape(-1)
    slot_valid = jnp.sum(recv_pick, axis=2).reshape(-1)
    free = jnp.einsum(
        "skt,tn->skn",
        panels.reshape(per_dev, 3 * block_len, spectral),
        table,
        preferred_element_type=jnp.float32,
    )
    free = free.reshape(-1, 3, block_len, NSTEP)
    force = jnp.einsum("cij,scjn->scin", coupling, free, precision=lax.Precision.HIGHEST)
    own = force.reshape(force.shape[0], 3 * block_len * NSTEP)
    outgoing = jnp.dot(send_pick.astype(jnp.float32), own, precision=lax.Precision.HIGHEST)
    outgoing = outgoing.reshape(width_gy, capacity, 3 * block_len * NSTEP)
    forces = lax.all_to_all(outgoing, "gy", split_axis=0, concat_axis=0, tiled=True)
    placing = (
        (slot_block[:, None] == jnp.arange(nblocks, dtype=jnp.int32)[None, :])
        & (slot_valid[:, None] > 0)
    ).astype(jnp.float32)
    gathered = jnp.einsum(
        "sb,sf->bf",
        placing,
        forces.reshape(width_gy * capacity, -1),
        precision=lax.Precision.HIGHEST,
    )
    gathered = gathered.reshape(size_x, size_y, zblocks, 3, block_len, NSTEP)
    drive_all = jnp.transpose(gathered, (5, 3, 0, 1, 2, 4)).reshape(
        NSTEP, 3, size_x, size_y, size_z
    )
    layers = jnp.arange(layer_speed.shape[0], dtype=jnp.int32)
    speed_z = jnp.sum(
        (layer_depth[None, :] == layers[:, None]).astype(jnp.float32) * layer_speed[:, None], axis=0
    )
    rate = lateral * speed_z[None, None, :]
    for step in range(NSTEP):
        padded = extended(u_now, (("gx", 1), ("gy", 2), ("gz", 3)), 1)
        laplace = neighbours(padded, u_now)
        u_next = 2.0 * u_now - u_prev + rate[None] * laplace + drive_all[step]
        u_prev = u_now
        u_now = u_next
    return (u_now, u_prev)


def solution(mesh):
    in_specs = (
        P(None, "gx", "gy", "gz"),
        P(None, "gx", "gy", "gz"),
        P("gx", "gz", "gy", None, None),
        P("gx", "gz", None, None),
        P("gx", "gz", None),
        P(),
        P("gz"),
        P(),
        P("gx", "gy", "gz"),
    )
    out_specs = (P(None, "gx", "gy", "gz"), P(None, "gx", "gy", "gz"))
    return jax.shard_map(
        per_device, mesh=mesh, in_specs=in_specs, out_specs=out_specs, check_vma=False
    )
```

profile of v0, /device:TPU:260, one launch (start us, length us, event | category | flops | bytes accessed | tf_op | source)
XLA Modules:
  0.0 218.7 jit_solution(6179045116059907670)
XLA Ops:
  5.0 12.1 %all-to-all-start = ((f32[24,2,192]{2,1,0:T(2,128)}), f32[24,2,192]{2,1,0:T(2,128)S(1)}, u32[]{:S(2)}, u32[]{:S(2)}) async-start(f32[24,2,192]{2,1,0:T(2,128)} %copy.96), calls=%async_computation | async-start | bytes 98304 | tf_op jit(solution)/shard_map/all_to_all | solution.py:80
  17.9 3.5 %collective-permute-start.1 = (f32[3,1,16,128]{3,2,1,0:T(8,128)S(1)}, f32[3,1,16,128]{3,2,1,0:T(8,128)S(1)}, u32[]{:S(2)}, u32[]{:S(2)}) collective-permute-start(f32[3,1,16,128]{3,2,1,0:T(8,128)S(1)} %get-tuple-element.31), channel_id=1, source_target_pairs={{0,48},{48,96},{96,144},{144,192},{192,240},{240,288},{288,336},{3... | collective-permute-start | bytes 73736 | tf_op jit(solution)/shard_map/ppermute | solution.py:16
  21.4 6.0 %collective-permute-start = (f32[3,1,16,128]{3,2,1,0:T(8,128)S(1)}, f32[3,1,16,128]{3,2,1,0:T(8,128)S(1)}, u32[]{:S(2)}, u32[]{:S(2)}) collective-permute-start(f32[3,1,16,128]{3,2,1,0:T(8,128)S(1)} %get-tuple-element.30), channel_id=1, source_target_pairs={{48,0},{96,48},{144,96},{192,144},{240,192},{288,240},{336,288},{3... | collective-permute-start | bytes 73736 | tf_op jit(solution)/shard_map/ppermute | solution.py:17
  31.8 1.9 collective-permute-start.2
  33.8 2.4 %collective-permute-start.3 = (f32[3,18,1,128]{3,2,1,0:T(1,128)S(1)}, f32[3,18,1,128]{3,2,1,0:T(1,128)S(1)}, u32[]{:S(2)}, u32[]{:S(2)}) collective-permute-start(f32[3,18,1,128]{3,2,1,0:T(1,128)S(1)} %get-tuple-element.22), channel_id=1, source_target_pairs={{0,2},{2,4},{4,6},{6,8},{8,10},{10,12},{12,14},{14,16},{16,18},{18... | collective-permute-start | bytes 82952 | tf_op jit(solution)/shard_map/ppermute | solution.py:16
  36.2 3.9 %collective-permute-done.3 = f32[3,18,1,128]{3,2,1,0:T(1,128)S(1)} collective-permute-done((f32[3,18,1,128]{3,2,1,0:T(1,128)S(1)}, f32[3,18,1,128]{3,2,1,0:T(1,128)S(1)}, u32[]{:S(2)}, u32[]{:S(2)}) %collective-permute-start.3) | collective-permute-done | bytes 27680 | tf_op jit(solution)/shard_map/ppermute | solution.py:16
  43.3 4.5 %collective-permute-start.5 = (f32[3,18,18,1]{2,3,1,0:T(1,128)S(1)}, f32[3,18,18,1]{2,3,1,0:T(1,128)S(1)}, u32[]{:S(2)}, u32[]{:S(2)}) collective-permute-start(f32[3,18,18,1]{2,3,1,0:T(1,128)S(1)} %copy.85), channel_id=1, source_target_pairs={{0,1},{2,3},{4,5},{6,7},{8,9},{10,11},{12,13},{14,15},{16,17},{18,... | collective-permute-start | bytes 11672 | tf_op jit(solution)/shard_map/ppermute | solution.py:16
  51.0 8.1 %convolution_bitcast_fusion = f32[4,3,16,16,8,16]{5,3,0,1,4,2:T(8,128)} fusion(s32[16,16,8]{1,2,0:T(8,128)S(1)} %multiply_add_fusion, s32[48]{0:T(128)S(1)} %eq.138, pred[48]{0:T(512)(128)(4,1)S(1)} %gt.16, f32[3,16,4,48,1,1]{3,2,1,0,5,4:T(4,128)S(1)} %bitcast.42), kind=kOutput, calls=%fused_computation | convolution fusion | flops 226689024 | bytes 1618160 | tf_op jit(solution)/shard_map/sb,sf->bf/dot_general | solution.py:85
  59.0 8.7 %fusion.59 = (f32[1,3,16,16,8,16]{5,3,0,1,4,2:T(8,128)S(1)}, f32[1,3,16,16,8,16]{5,3,0,1,4,2:T(8,128)S(1)}, f32[1,3,16,16,8,16]{5,3,0,1,4,2:T(8,128)}, f32[1,3,16,16,8,16]{5,3,0,1,4,2:T(8,128)}) fusion(f32[4,3,16,16,8,16]{5,3,0,1,4,2:T(8,128)} %convolution_bitcast_fusion), kind=kLoop, calls=%fused_computation.162 | loop fusion | bytes 3145728 | tf_op jit(solution)/shard_map/slice | solution.py:103
  67.7 3.1 %copy.99 = f32[1,3,16,16,8,16]{5,4,3,2,1,0:T(8,128)} copy(f32[1,3,16,16,8,16]{5,3,0,1,4,2:T(8,128)S(1)} %get-tuple-element.4) | data formatting | bytes 786432 | tf_op jit(solution)/shard_map/slice | solution.py:103
  70.8 3.1 %squeeze.15 = f32[3,16,16,128]{3,2,1,0:T(8,128)} reshape(f32[1,3,16,16,8,16]{5,4,3,2,1,0:T(8,128)} %copy.99) | data formatting | bytes 786432 | tf_op jit(solution)/shard_map/squeeze | solution.py:103
  73.8 3.0 %fusion.38 = f32[3,16,16,128]{3,2,1,0:T(8,128)S(1)} fusion(f32[3,16,16,128]{3,2,1,0:T(8,128)} %squeeze.15, f32[3,18,18,1]{3,2,1,0:T(8,128)} %copy.86, f32[3,18,1,128]{3,2,1,0:T(1,128)} %copy-done.24, f32[3,18,16,128]{3,2,1,0:T(8,128)} %copy-done.7, f32[3,18,1,128]{3,2,1,0:T(1,128)} %copy-done.25, f32[3,18,18,1]{3,2,1,0:T(8,128)} %copy.84, ...), kind=kLoop, calls=%fused_computation.101 | loop fusion | flops 2162688 | bytes 2258528 | tf_op jit(solution)/shard_map/add | solution.py:103
  76.9 4.9 %collective-permute-start.6 = (f32[3,1,16,128]{3,2,1,0:T(8,128)S(1)}, f32[3,1,16,128]{3,2,1,0:T(8,128)S(1)}, u32[]{:S(2)}, u32[]{:S(2)}) collective-permute-start(f32[3,1,16,128]{3,2,1,0:T(8,128)S(1)} %get-tuple-element.29), channel_id=1, source_target_pairs={{48,0},{96,48},{144,96},{192,144},{240,192},{288,240},{336,288},{3... | collective-permute-start | bytes 73736 | tf_op jit(solution)/shard_map/ppermute | solution.py:17
  81.8 1.9 collective-permute-start.7
  83.7 7.4 %collective-permute-done.7 = f32[3,1,16,128]{3,2,1,0:T(8,128)S(1)} collective-permute-done((f32[3,1,16,128]{3,2,1,0:T(8,128)S(1)}, f32[3,1,16,128]{3,2,1,0:T(8,128)S(1)}, u32[]{:S(2)}, u32[]{:S(2)}) %collective-permute-start.7) | collective-permute-done | bytes 24608 | tf_op jit(solution)/shard_map/ppermute | solution.py:16
  91.2 1.9 collective-permute-start.8
  93.1 2.4 %collective-permute-start.9 = (f32[3,18,1,128]{3,2,1,0:T(1,128)S(1)}, f32[3,18,1,128]{3,2,1,0:T(1,128)S(1)}, u32[]{:S(2)}, u32[]{:S(2)}) collective-permute-start(f32[3,18,1,128]{3,2,1,0:T(1,128)S(1)} %get-tuple-element.20), channel_id=1, source_target_pairs={{0,2},{2,4},{4,6},{6,8},{8,10},{10,12},{12,14},{14,16},{16,18},{18... | collective-permute-start | bytes 82952 | tf_op jit(solution)/shard_map/ppermute | solution.py:16
  95.5 4.0 %collective-permute-done.9 = f32[3,18,1,128]{3,2,1,0:T(1,128)S(1)} collective-permute-done((f32[3,18,1,128]{3,2,1,0:T(1,128)S(1)}, f32[3,18,1,128]{3,2,1,0:T(1,128)S(1)}, u32[]{:S(2)}, u32[]{:S(2)}) %collective-permute-start.9) | collective-permute-done | bytes 27680 | tf_op jit(solution)/shard_map/ppermute | solution.py:16
  101.5 2.1 copy.100
  104.9 2.1 copy.102
  107.0 5.8 %collective-permute-start.11 = (f32[3,18,18,1]{2,3,1,0:T(1,128)}, f32[3,18,18,1]{2,3,1,0:T(1,128)}, u32[]{:S(2)}, u32[]{:S(2)}) collective-permute-start(f32[3,18,18,1]{2,3,1,0:T(1,128)} %copy.102), channel_id=1, source_target_pairs={{0,1},{2,3},{4,5},{6,7},{8,9},{10,11},{12,13},{14,15},{16,17},{18,... | collective-permute-start | bytes 11672 | tf_op jit(solution)/shard_map/ppermute | solution.py:16
  112.8 5.0 %copy.104 = f32[1,3,16,16,8,16]{5,4,3,2,1,0:T(8,128)} copy(f32[1,3,16,16,8,16]{5,3,0,1,4,2:T(8,128)} %get-tuple-element.7) | data formatting | bytes 786432 | tf_op jit(solution)/shard_map/slice | solution.py:103
  117.7 3.1 %squeeze.16 = f32[3,16,16,128]{3,2,1,0:T(8,128)} reshape(f32[1,3,16,16,8,16]{5,4,3,2,1,0:T(8,128)} %copy.104) | data formatting | bytes 786432 | tf_op jit(solution)/shard_map/squeeze | solution.py:103
  120.8 2.0 copy.101
  122.8 2.0 copy.103
  124.9 3.4 %fusion.29 = f32[3,16,16,128]{3,2,1,0:T(8,128)S(1)} fusion(f32[3,16,16,128]{3,2,1,0:T(8,128)} %squeeze.16, f32[3,18,18,1]{3,2,1,0:T(8,128)} %copy.103, f32[3,18,1,128]{3,2,1,0:T(1,128)} %copy-done.19, f32[3,18,1,128]{3,2,1,0:T(1,128)} %copy-done.23, f32[3,1,16,128]{3,2,1,0:T(8,128)} %copy-done.11, f32[3,16,16,128]{3,2,1,0:T(8,128)} %copy-done.3, ...), kind=kLoop, calls=%fused_computation.74 | loop fusion | flops 2949120 | bytes 1816160 | tf_op jit(solution)/shard_map/add | solution.py:103
  128.3 1.9 collective-permute-start.12
  130.3 3.9 %collective-permute-start.13 = (f32[3,1,16,128]{3,2,1,0:T(8,128)S(1)}, f32[3,1,16,128]{3,2,1,0:T(8,128)S(1)}, u32[]{:S(2)}, u32[]{:S(2)}) collective-permute-start(f32[3,1,16,128]{3,2,1,0:T(8,128)S(1)} %get-tuple-element.26), channel_id=1, source_target_pairs={{0,48},{48,96},{96,144},{144,192},{192,240},{240,288},{288,336},{3... | collective-permute-start | bytes 73736 | tf_op jit(solution)/shard_map/ppermute | solution.py:16
  134.2 5.4 %collective-permute-done.13 = f32[3,1,16,128]{3,2,1,0:T(8,128)S(1)} collective-permute-done((f32[3,1,16,128]{3,2,1,0:T(8,128)S(1)}, f32[3,1,16,128]{3,2,1,0:T(8,128)S(1)}, u32[]{:S(2)}, u32[]{:S(2)}) %collective-permute-start.13) | collective-permute-done | bytes 24608 | tf_op jit(solution)/shard_map/ppermute | solution.py:16
  141.6 2.4 %collective-permute-start.15 = (f32[3,18,1,128]{3,2,1,0:T(1,128)S(1)}, f32[3,18,1,128]{3,2,1,0:T(1,128)S(1)}, u32[]{:S(2)}, u32[]{:S(2)}) collective-permute-start(f32[3,18,1,128]{3,2,1,0:T(1,128)S(1)} %get-tuple-element.18), channel_id=1, source_target_pairs={{0,2},{2,4},{4,6},{6,8},{8,10},{10,12},{12,14},{14,16},{16,18},{18... | collective-permute-start | bytes 82952 | tf_op jit(solution)/shard_map/ppermute | solution.py:16
  144.0 4.0 %collective-permute-done.15 = f32[3,18,1,128]{3,2,1,0:T(1,128)S(1)} collective-permute-done((f32[3,18,1,128]{3,2,1,0:T(1,128)S(1)}, f32[3,18,1,128]{3,2,1,0:T(1,128)S(1)}, u32[]{:S(2)}, u32[]{:S(2)}) %collective-permute-start.15) | collective-permute-done | bytes 27680 | tf_op jit(solution)/shard_map/ppermute | solution.py:16
  149.9 2.1 copy.105
  153.3 2.1 copy.107
  155.4 5.7 %collective-permute-start.17 = (f32[3,18,18,1]{2,3,1,0:T(1,128)}, f32[3,18,18,1]{2,3,1,0:T(1,128)}, u32[]{:S(2)}, u32[]{:S(2)}) collective-permute-start(f32[3,18,18,1]{2,3,1,0:T(1,128)} %copy.107), channel_id=1, source_target_pairs={{0,1},{2,3},{4,5},{6,7},{8,9},{10,11},{12,13},{14,15},{16,17},{18,... | collective-permute-start | bytes 11672 | tf_op jit(solution)/shard_map/ppermute | solution.py:16
  161.2 5.0 %copy.109 = f32[1,3,16,16,8,16]{5,4,3,2,1,0:T(8,128)} copy(f32[1,3,16,16,8,16]{5,3,0,1,4,2:T(8,128)} %get-tuple-element.6) | data formatting | bytes 786432 | tf_op jit(solution)/shard_map/slice | solution.py:103
  166.1 3.1 %squeeze.17 = f32[3,16,16,128]{3,2,1,0:T(8,128)} reshape(f32[1,3,16,16,8,16]{5,4,3,2,1,0:T(8,128)} %copy.109) | data formatting | bytes 786432 | tf_op jit(solution)/shard_map/squeeze | solution.py:103
  169.2 2.0 copy.106
  171.2 2.0 copy.108
  173.2 3.2 %fusion.20 = f32[3,16,16,128]{3,2,1,0:T(8,128)S(1)} fusion(f32[3,16,16,128]{3,2,1,0:T(8,128)} %squeeze.17, f32[3,18,18,1]{3,2,1,0:T(8,128)} %copy.108, f32[3,18,1,128]{3,2,1,0:T(1,128)} %copy-done.18, f32[3,18,1,128]{3,2,1,0:T(1,128)} %copy-done.22, f32[3,1,16,128]{3,2,1,0:T(8,128)} %copy-done.10, f32[3,16,16,128]{3,2,1,0:T(8,128)} %copy-done.1, ...), kind=kLoop, calls=%fused_computation.47 | loop fusion | flops 2949120 | bytes 1816160 | tf_op jit(solution)/shard_map/add | solution.py:103
  178.4 3.9 %collective-permute-start.19 = (f32[3,1,16,128]{3,2,1,0:T(8,128)S(1)}, f32[3,1,16,128]{3,2,1,0:T(8,128)S(1)}, u32[]{:S(2)}, u32[]{:S(2)}) collective-permute-start(f32[3,1,16,128]{3,2,1,0:T(8,128)S(1)} %get-tuple-element.24), channel_id=1, source_target_pairs={{0,48},{48,96},{96,144},{144,192},{192,240},{240,288},{288,336},{3... | collective-permute-start | bytes 73736 | tf_op jit(solution)/shard_map/ppermute | solution.py:16
  182.4 5.4 %collective-permute-done.19 = f32[3,1,16,128]{3,2,1,0:T(8,128)S(1)} collective-permute-done((f32[3,1,16,128]{3,2,1,0:T(8,128)S(1)}, f32[3,1,16,128]{3,2,1,0:T(8,128)S(1)}, u32[]{:S(2)}, u32[]{:S(2)}) %collective-permute-start.19) | collective-permute-done | bytes 24608 | tf_op jit(solution)/shard_map/ppermute | solution.py:16
  189.8 2.4 %collective-permute-start.21 = (f32[3,18,1,128]{3,2,1,0:T(1,128)S(1)}, f32[3,18,1,128]{3,2,1,0:T(1,128)S(1)}, u32[]{:S(2)}, u32[]{:S(2)}) collective-permute-start(f32[3,18,1,128]{3,2,1,0:T(1,128)S(1)} %get-tuple-element.16), channel_id=1, source_target_pairs={{0,2},{2,4},{4,6},{6,8},{8,10},{10,12},{12,14},{14,16},{16,18},{18... | collective-permute-start | bytes 82952 | tf_op jit(solution)/shard_map/ppermute | solution.py:16
  192.2 4.0 %collective-permute-done.21 = f32[3,18,1,128]{3,2,1,0:T(1,128)S(1)} collective-permute-done((f32[3,18,1,128]{3,2,1,0:T(1,128)S(1)}, f32[3,18,1,128]{3,2,1,0:T(1,128)S(1)}, u32[]{:S(2)}, u32[]{:S(2)}) %collective-permute-start.21) | collective-permute-done | bytes 27680 | tf_op jit(solution)/shard_map/ppermute | solution.py:16
  198.1 2.1 copy.110
  201.5 2.1 copy.112
  203.6 5.7 %collective-permute-start.23 = (f32[3,18,18,1]{2,3,1,0:T(1,128)}, f32[3,18,18,1]{2,3,1,0:T(1,128)}, u32[]{:S(2)}, u32[]{:S(2)}) collective-permute-start(f32[3,18,18,1]{2,3,1,0:T(1,128)} %copy.112), channel_id=1, source_target_pairs={{0,1},{2,3},{4,5},{6,7},{8,9},{10,11},{12,13},{14,15},{16,17},{18,... | collective-permute-start | bytes 11672 | tf_op jit(solution)/shard_map/ppermute | solution.py:16
  209.3 3.1 %copy.114 = f32[1,3,16,16,8,16]{5,4,3,2,1,0:T(8,128)} copy(f32[1,3,16,16,8,16]{5,3,0,1,4,2:T(8,128)S(1)} %get-tuple-element.5) | data formatting | bytes 786432 | tf_op jit(solution)/shard_map/slice | solution.py:103
  212.5 2.5 %squeeze.18 = f32[3,16,16,128]{3,2,1,0:T(8,128)S(1)} reshape(f32[1,3,16,16,8,16]{5,4,3,2,1,0:T(8,128)} %copy.114) | data formatting | bytes 786432 | tf_op jit(solution)/shard_map/squeeze | solution.py:103
  (140 shorter events, 35.1 us)
Async XLA Ops:
  5.0 45.8 %all-to-all-start = ((f32[24,2,192]{2,1,0:T(2,128)}), f32[24,2,192]{2,1,0:T(2,128)S(1)}, u32[]{:S(2)}, u32[]{:S(2)}) async-start(f32[24,2,192]{2,1,0:T(2,128)} %copy.96), calls=%async_computation | async-start | bytes 98304 | tf_op jit(solution)/shard_map/all_to_all | solution.py:80
  17.9 12.8 %collective-permute-start.1 = (f32[3,1,16,128]{3,2,1,0:T(8,128)S(1)}, f32[3,1,16,128]{3,2,1,0:T(8,128)S(1)}, u32[]{:S(2)}, u32[]{:S(2)}) collective-permute-start(f32[3,1,16,128]{3,2,1,0:T(8,128)S(1)} %get-tuple-element.31), channel_id=1, source_target_pairs={{0,48},{48,96},{96,144},{144,192},{192,240},{240,288},{288,336},{3... | collective-permute-start | bytes 73736 | tf_op jit(solution)/shard_map/ppermute | solution.py:16
  21.4 10.4 %collective-permute-start = (f32[3,1,16,128]{3,2,1,0:T(8,128)S(1)}, f32[3,1,16,128]{3,2,1,0:T(8,128)S(1)}, u32[]{:S(2)}, u32[]{:S(2)}) collective-permute-start(f32[3,1,16,128]{3,2,1,0:T(8,128)S(1)} %get-tuple-element.30), channel_id=1, source_target_pairs={{48,0},{96,48},{144,96},{192,144},{240,192},{288,240},{336,288},{3... | collective-permute-start | bytes 73736 | tf_op jit(solution)/shard_map/ppermute | solution.py:17
  30.7 9.5 %copy-start.26 = (f32[3,1,16,128]{3,2,1,0:T(8,128)}, f32[3,1,16,128]{3,2,1,0:T(8,128)S(1)}, u32[]{:S(2)}) copy-start(f32[3,1,16,128]{3,2,1,0:T(8,128)S(1)} %collective-permute-done.1) | copy-start | bytes 73732
  31.8 8.4 %copy-start.27 = (f32[3,1,16,128]{3,2,1,0:T(8,128)}, f32[3,1,16,128]{3,2,1,0:T(8,128)S(1)}, u32[]{:S(2)}) copy-start(f32[3,1,16,128]{3,2,1,0:T(8,128)S(1)} %collective-permute-done) | copy-start | bytes 73732
  31.8 8.4 %copy-start.7 = (f32[3,18,16,128]{3,2,1,0:T(8,128)}, f32[3,18,16,128]{3,2,1,0:T(8,128)S(1)}, u32[]{:S(2)}) copy-start(f32[3,18,16,128]{3,2,1,0:T(8,128)S(1)} %constant_dynamic-update-slice_fusion) | copy-start | bytes 1327108
  31.8 4.4 %collective-permute-start.2 = (f32[3,18,1,128]{3,2,1,0:T(1,128)S(1)}, f32[3,18,1,128]{3,2,1,0:T(1,128)S(1)}, u32[]{:S(2)}, u32[]{:S(2)}) collective-permute-start(f32[3,18,1,128]{3,2,1,0:T(1,128)S(1)} %get-tuple-element.23), channel_id=1, source_target_pairs={{2,0},{4,2},{6,4},{8,6},{10,8},{12,10},{14,12},{16,14},{18,16},{20... | collective-permute-start | bytes 82952 | tf_op jit(solution)/shard_map/ppermute | solution.py:17
  33.8 6.4 %collective-permute-start.3 = (f32[3,18,1,128]{3,2,1,0:T(1,128)S(1)}, f32[3,18,1,128]{3,2,1,0:T(1,128)S(1)}, u32[]{:S(2)}, u32[]{:S(2)}) collective-permute-start(f32[3,18,1,128]{3,2,1,0:T(1,128)S(1)} %get-tuple-element.22), channel_id=1, source_target_pairs={{0,2},{2,4},{4,6},{6,8},{8,10},{10,12},{12,14},{14,16},{16,18},{18... | collective-permute-start | bytes 82952 | tf_op jit(solution)/shard_map/ppermute | solution.py:16
  36.2 4.0 %copy-start.24 = (f32[3,18,1,128]{3,2,1,0:T(1,128)}, f32[3,18,1,128]{3,2,1,0:T(1,128)S(1)}, u32[]{:S(2)}) copy-start(f32[3,18,1,128]{3,2,1,0:T(1,128)S(1)} %collective-permute-done.2) | copy-start | bytes 82948
  41.6 6.7 %collective-permute-start.4 = (f32[3,18,18,1]{2,3,1,0:T(1,128)S(1)}, f32[3,18,18,1]{2,3,1,0:T(1,128)S(1)}, u32[]{:S(2)}, u32[]{:S(2)}) collective-permute-start(f32[3,18,18,1]{2,3,1,0:T(1,128)S(1)} %copy.83), channel_id=1, source_target_pairs={{1,0},{3,2},{5,4},{7,6},{9,8},{11,10},{13,12},{15,14},{17,16},{19,... | collective-permute-start | bytes 11672 | tf_op jit(solution)/shard_map/ppermute | solution.py:17
  43.3 6.3 %collective-permute-start.5 = (f32[3,18,18,1]{2,3,1,0:T(1,128)S(1)}, f32[3,18,18,1]{2,3,1,0:T(1,128)S(1)}, u32[]{:S(2)}, u32[]{:S(2)}) collective-permute-start(f32[3,18,18,1]{2,3,1,0:T(1,128)S(1)} %copy.85), channel_id=1, source_target_pairs={{0,1},{2,3},{4,5},{6,7},{8,9},{10,11},{12,13},{14,15},{16,17},{18,... | collective-permute-start | bytes 11672 | tf_op jit(solution)/shard_map/ppermute | solution.py:16
  76.8 22.7 %copy-start.3 = (f32[3,16,16,128]{3,2,1,0:T(8,128)}, f32[3,16,16,128]{3,2,1,0:T(8,128)S(1)}, u32[]{:S(2)}) copy-start(f32[3,16,16,128]{3,2,1,0:T(8,128)S(1)} %fusion.38) | copy-start | bytes 1179652
  76.9 6.9 %collective-permute-start.6 = (f32[3,1,16,128]{3,2,1,0:T(8,128)S(1)}, f32[3,1,16,128]{3,2,1,0:T(8,128)S(1)}, u32[]{:S(2)}, u32[]{:S(2)}) collective-permute-start(f32[3,1,16,128]{3,2,1,0:T(8,128)S(1)} %get-tuple-element.29), channel_id=1, source_target_pairs={{48,0},{96,48},{144,96},{192,144},{240,192},{288,240},{336,288},{3... | collective-permute-start | bytes 73736 | tf_op jit(solution)/shard_map/ppermute | solution.py:17
  81.8 9.3 %collective-permute-start.7 = (f32[3,1,16,128]{3,2,1,0:T(8,128)S(1)}, f32[3,1,16,128]{3,2,1,0:T(8,128)S(1)}, u32[]{:S(2)}, u32[]{:S(2)}) collective-permute-start(f32[3,1,16,128]{3,2,1,0:T(8,128)S(1)} %get-tuple-element.28), channel_id=1, source_target_pairs={{0,48},{48,96},{96,144},{144,192},{192,240},{240,288},{288,336},{3... | collective-permute-start | bytes 73736 | tf_op jit(solution)/shard_map/ppermute | solution.py:16
  83.7 15.8 %copy-start.11 = (f32[3,1,16,128]{3,2,1,0:T(8,128)}, f32[3,1,16,128]{3,2,1,0:T(8,128)S(1)}, u32[]{:S(2)}) copy-start(f32[3,1,16,128]{3,2,1,0:T(8,128)S(1)} %collective-permute-done.6) | copy-start | bytes 73732
  91.1 8.4 %copy-start.15 = (f32[3,1,16,128]{3,2,1,0:T(8,128)}, f32[3,1,16,128]{3,2,1,0:T(8,128)S(1)}, u32[]{:S(2)}) copy-start(f32[3,1,16,128]{3,2,1,0:T(8,128)S(1)} %collective-permute-done.7) | copy-start | bytes 73732
  91.2 4.3 %collective-permute-start.8 = (f32[3,18,1,128]{3,2,1,0:T(1,128)S(1)}, f32[3,18,1,128]{3,2,1,0:T(1,128)S(1)}, u32[]{:S(2)}, u32[]{:S(2)}) collective-permute-start(f32[3,18,1,128]{3,2,1,0:T(1,128)S(1)} %get-tuple-element.21), channel_id=1, source_target_pairs={{2,0},{4,2},{6,4},{8,6},{10,8},{12,10},{14,12},{16,14},{18,16},{20... | collective-permute-start | bytes 82952 | tf_op jit(solution)/shard_map/ppermute | solution.py:17
  93.1 6.4 %collective-permute-start.9 = (f32[3,18,1,128]{3,2,1,0:T(1,128)S(1)}, f32[3,18,1,128]{3,2,1,0:T(1,128)S(1)}, u32[]{:S(2)}, u32[]{:S(2)}) collective-permute-start(f32[3,18,1,128]{3,2,1,0:T(1,128)S(1)} %get-tuple-element.20), channel_id=1, source_target_pairs={{0,2},{2,4},{4,6},{6,8},{8,10},{10,12},{12,14},{14,16},{16,18},{18... | collective-permute-start | bytes 82952 | tf_op jit(solution)/shard_map/ppermute | solution.py:16
  95.5 4.0 %copy-start.19 = (f32[3,18,1,128]{3,2,1,0:T(1,128)}, f32[3,18,1,128]{3,2,1,0:T(1,128)S(1)}, u32[]{:S(2)}) copy-start(f32[3,18,1,128]{3,2,1,0:T(1,128)S(1)} %collective-permute-done.8) | copy-start | bytes 82948
  103.6 17.2 %collective-permute-start.10 = (f32[3,18,18,1]{2,3,1,0:T(1,128)}, f32[3,18,18,1]{2,3,1,0:T(1,128)}, u32[]{:S(2)}, u32[]{:S(2)}) collective-permute-start(f32[3,18,18,1]{2,3,1,0:T(1,128)} %copy.100), channel_id=1, source_target_pairs={{1,0},{3,2},{5,4},{7,6},{9,8},{11,10},{13,12},{15,14},{17,16},{19,... | collective-permute-start | bytes 11672 | tf_op jit(solution)/shard_map/ppermute | solution.py:17
  107.0 15.8 %collective-permute-start.11 = (f32[3,18,18,1]{2,3,1,0:T(1,128)}, f32[3,18,18,1]{2,3,1,0:T(1,128)}, u32[]{:S(2)}, u32[]{:S(2)}) collective-permute-start(f32[3,18,18,1]{2,3,1,0:T(1,128)} %copy.102), channel_id=1, source_target_pairs={{0,1},{2,3},{4,5},{6,7},{8,9},{10,11},{12,13},{14,15},{16,17},{18,... | collective-permute-start | bytes 11672 | tf_op jit(solution)/shard_map/ppermute | solution.py:16
  128.3 19.7 %copy-start.1 = (f32[3,16,16,128]{3,2,1,0:T(8,128)}, f32[3,16,16,128]{3,2,1,0:T(8,128)S(1)}, u32[]{:S(2)}) copy-start(f32[3,16,16,128]{3,2,1,0:T(8,128)S(1)} %fusion.29) | copy-start | bytes 1179652
  128.3 5.9 %collective-permute-start.12 = (f32[3,1,16,128]{3,2,1,0:T(8,128)S(1)}, f32[3,1,16,128]{3,2,1,0:T(8,128)S(1)}, u32[]{:S(2)}, u32[]{:S(2)}) collective-permute-start(f32[3,1,16,128]{3,2,1,0:T(8,128)S(1)} %get-tuple-element.27), channel_id=1, source_target_pairs={{48,0},{96,48},{144,96},{192,144},{240,192},{288,240},{336,288},{3... | collective-permute-start | bytes 73736 | tf_op jit(solution)/shard_map/ppermute | solution.py:17
  130.3 9.3 %collective-permute-start.13 = (f32[3,1,16,128]{3,2,1,0:T(8,128)S(1)}, f32[3,1,16,128]{3,2,1,0:T(8,128)S(1)}, u32[]{:S(2)}, u32[]{:S(2)}) collective-permute-start(f32[3,1,16,128]{3,2,1,0:T(8,128)S(1)} %get-tuple-element.26), channel_id=1, source_target_pairs={{0,48},{48,96},{96,144},{144,192},{192,240},{240,288},{288,336},{3... | collective-permute-start | bytes 73736 | tf_op jit(solution)/shard_map/ppermute | solution.py:16
  134.2 13.8 %copy-start.10 = (f32[3,1,16,128]{3,2,1,0:T(8,128)}, f32[3,1,16,128]{3,2,1,0:T(8,128)S(1)}, u32[]{:S(2)}) copy-start(f32[3,1,16,128]{3,2,1,0:T(8,128)S(1)} %collective-permute-done.12) | copy-start | bytes 73732
  139.6 8.4 %copy-start.14 = (f32[3,1,16,128]{3,2,1,0:T(8,128)}, f32[3,1,16,128]{3,2,1,0:T(8,128)S(1)}, u32[]{:S(2)}) copy-start(f32[3,1,16,128]{3,2,1,0:T(8,128)S(1)} %collective-permute-done.13) | copy-start | bytes 73732
  139.6 4.3 %collective-permute-start.14 = (f32[3,18,1,128]{3,2,1,0:T(1,128)S(1)}, f32[3,18,1,128]{3,2,1,0:T(1,128)S(1)}, u32[]{:S(2)}, u32[]{:S(2)}) collective-permute-start(f32[3,18,1,128]{3,2,1,0:T(1,128)S(1)} %get-tuple-element.19), channel_id=1, source_target_pairs={{2,0},{4,2},{6,4},{8,6},{10,8},{12,10},{14,12},{16,14},{18,16},{20... | collective-permute-start | bytes 82952 | tf_op jit(solution)/shard_map/ppermute | solution.py:17
  141.6 6.4 %collective-permute-start.15 = (f32[3,18,1,128]{3,2,1,0:T(1,128)S(1)}, f32[3,18,1,128]{3,2,1,0:T(1,128)S(1)}, u32[]{:S(2)}, u32[]{:S(2)}) collective-permute-start(f32[3,18,1,128]{3,2,1,0:T(1,128)S(1)} %get-tuple-element.18), channel_id=1, source_target_pairs={{0,2},{2,4},{4,6},{6,8},{8,10},{10,12},{12,14},{14,16},{16,18},{18... | collective-permute-start | bytes 82952 | tf_op jit(solution)/shard_map/ppermute | solution.py:16
  144.0 4.0 %copy-start.18 = (f32[3,18,1,128]{3,2,1,0:T(1,128)}, f32[3,18,1,128]{3,2,1,0:T(1,128)S(1)}, u32[]{:S(2)}) copy-start(f32[3,18,1,128]{3,2,1,0:T(1,128)S(1)} %collective-permute-done.14) | copy-start | bytes 82948
  152.1 17.1 %collective-permute-start.16 = (f32[3,18,18,1]{2,3,1,0:T(1,128)}, f32[3,18,18,1]{2,3,1,0:T(1,128)}, u32[]{:S(2)}, u32[]{:S(2)}) collective-permute-start(f32[3,18,18,1]{2,3,1,0:T(1,128)} %copy.105), channel_id=1, source_target_pairs={{1,0},{3,2},{5,4},{7,6},{9,8},{11,10},{13,12},{15,14},{17,16},{19,... | collective-permute-start | bytes 11672 | tf_op jit(solution)/shard_map/ppermute | solution.py:17
  155.4 15.8 %collective-permute-start.17 = (f32[3,18,18,1]{2,3,1,0:T(1,128)}, f32[3,18,18,1]{2,3,1,0:T(1,128)}, u32[]{:S(2)}, u32[]{:S(2)}) collective-permute-start(f32[3,18,18,1]{2,3,1,0:T(1,128)} %copy.107), channel_id=1, source_target_pairs={{0,1},{2,3},{4,5},{6,7},{8,9},{10,11},{12,13},{14,15},{16,17},{18,... | collective-permute-start | bytes 11672 | tf_op jit(solution)/shard_map/ppermute | solution.py:16
  176.5 19.7 %copy-start.4 = (f32[3,16,16,128]{3,2,1,0:T(8,128)}, f32[3,16,16,128]{3,2,1,0:T(8,128)S(1)}, u32[]{:S(2)}) copy-start(f32[3,16,16,128]{3,2,1,0:T(8,128)S(1)} %fusion.20) | copy-start | bytes 1179652
  176.5 5.9 %collective-permute-start.18 = (f32[3,1,16,128]{3,2,1,0:T(8,128)S(1)}, f32[3,1,16,128]{3,2,1,0:T(8,128)S(1)}, u32[]{:S(2)}, u32[]{:S(2)}) collective-permute-start(f32[3,1,16,128]{3,2,1,0:T(8,128)S(1)} %get-tuple-element.25), channel_id=1, source_target_pairs={{48,0},{96,48},{144,96},{192,144},{240,192},{288,240},{336,288},{3... | collective-permute-start | bytes 73736 | tf_op jit(solution)/shard_map/ppermute | solution.py:17
  178.4 9.3 %collective-permute-start.19 = (f32[3,1,16,128]{3,2,1,0:T(8,128)S(1)}, f32[3,1,16,128]{3,2,1,0:T(8,128)S(1)}, u32[]{:S(2)}, u32[]{:S(2)}) collective-permute-start(f32[3,1,16,128]{3,2,1,0:T(8,128)S(1)} %get-tuple-element.24), channel_id=1, source_target_pairs={{0,48},{48,96},{96,144},{144,192},{192,240},{240,288},{288,336},{3... | collective-permute-start | bytes 73736 | tf_op jit(solution)/shard_map/ppermute | solution.py:16
  182.4 13.8 %copy-start.8 = (f32[3,1,16,128]{3,2,1,0:T(8,128)}, f32[3,1,16,128]{3,2,1,0:T(8,128)S(1)}, u32[]{:S(2)}) copy-start(f32[3,1,16,128]{3,2,1,0:T(8,128)S(1)} %collective-permute-done.18) | copy-start | bytes 73732
  187.8 8.4 %copy-start.12 = (f32[3,1,16,128]{3,2,1,0:T(8,128)}, f32[3,1,16,128]{3,2,1,0:T(8,128)S(1)}, u32[]{:S(2)}) copy-start(f32[3,1,16,128]{3,2,1,0:T(8,128)S(1)} %collective-permute-done.19) | copy-start | bytes 73732
  187.8 4.3 %collective-permute-start.20 = (f32[3,18,1,128]{3,2,1,0:T(1,128)S(1)}, f32[3,18,1,128]{3,2,1,0:T(1,128)S(1)}, u32[]{:S(2)}, u32[]{:S(2)}) collective-permute-start(f32[3,18,1,128]{3,2,1,0:T(1,128)S(1)} %get-tuple-element.17), channel_id=1, source_target_pairs={{2,0},{4,2},{6,4},{8,6},{10,8},{12,10},{14,12},{16,14},{18,16},{20... | collective-permute-start | bytes 82952 | tf_op jit(solution)/shard_map/ppermute | solution.py:17
  189.8 6.4 %collective-permute-start.21 = (f32[3,18,1,128]{3,2,1,0:T(1,128)S(1)}, f32[3,18,1,128]{3,2,1,0:T(1,128)S(1)}, u32[]{:S(2)}, u32[]{:S(2)}) collective-permute-start(f32[3,18,1,128]{3,2,1,0:T(1,128)S(1)} %get-tuple-element.16), channel_id=1, source_target_pairs={{0,2},{2,4},{4,6},{6,8},{8,10},{10,12},{12,14},{14,16},{16,18},{18... | collective-permute-start | bytes 82952 | tf_op jit(solution)/shard_map/ppermute | solution.py:16
  192.2 4.0 %copy-start.16 = (f32[3,18,1,128]{3,2,1,0:T(1,128)}, f32[3,18,1,128]{3,2,1,0:T(1,128)S(1)}, u32[]{:S(2)}) copy-start(f32[3,18,1,128]{3,2,1,0:T(1,128)S(1)} %collective-permute-done.20) | copy-start | bytes 82948
  200.2 14.7 %collective-permute-start.22 = (f32[3,18,18,1]{2,3,1,0:T(1,128)}, f32[3,18,18,1]{2,3,1,0:T(1,128)}, u32[]{:S(2)}, u32[]{:S(2)}) collective-permute-start(f32[3,18,18,1]{2,3,1,0:T(1,128)} %copy.110), channel_id=1, source_target_pairs={{1,0},{3,2},{5,4},{7,6},{9,8},{11,10},{13,12},{15,14},{17,16},{19,... | collective-permute-start | bytes 11672 | tf_op jit(solution)/shard_map/ppermute | solution.py:17
  203.6 12.5 %collective-permute-start.23 = (f32[3,18,18,1]{2,3,1,0:T(1,128)}, f32[3,18,18,1]{2,3,1,0:T(1,128)}, u32[]{:S(2)}, u32[]{:S(2)}) collective-permute-start(f32[3,18,18,1]{2,3,1,0:T(1,128)} %copy.112), channel_id=1, source_target_pairs={{0,1},{2,3},{4,5},{6,7},{8,9},{10,11},{12,13},{14,15},{16,17},{18,... | collective-permute-start | bytes 11672 | tf_op jit(solution)/shard_map/ppermute | solution.py:16
  212.4 4.9 %copy-start.2 = (f32[3,16,16,128]{3,2,1,0:T(8,128)S(1)}, f32[3,16,16,128]{3,2,1,0:T(8,128)}, u32[]{:S(2)}) copy-start(f32[3,16,16,128]{3,2,1,0:T(8,128)} %copy-done.1) | copy-start | bytes 1179652
  212.4 4.9 %copy-start.5 = (f32[3,16,16,128]{3,2,1,0:T(8,128)S(1)}, f32[3,16,16,128]{3,2,1,0:T(8,128)}, u32[]{:S(2)}) copy-start(f32[3,16,16,128]{3,2,1,0:T(8,128)} %copy-done.4) | copy-start | bytes 1179652
  212.4 4.9 %copy-start.6 = (f32[16,16,128]{2,1,0:T(8,128)S(1)}, f32[16,16,128]{2,1,0:T(8,128)}, u32[]{:S(2)}) copy-start(f32[16,16,128]{2,1,0:T(8,128)} %broadcast_multiply_fusion) | copy-start | bytes 393220
  212.4 4.9 %copy-start.9 = (f32[3,1,16,128]{3,2,1,0:T(8,128)S(1)}, f32[3,1,16,128]{3,2,1,0:T(8,128)}, u32[]{:S(2)}) copy-start(f32[3,1,16,128]{3,2,1,0:T(8,128)} %copy-done.8) | copy-start | bytes 73732
  212.4 4.9 %copy-start.13 = (f32[3,1,16,128]{3,2,1,0:T(8,128)S(1)}, f32[3,1,16,128]{3,2,1,0:T(8,128)}, u32[]{:S(2)}) copy-start(f32[3,1,16,128]{3,2,1,0:T(8,128)} %copy-done.12) | copy-start | bytes 73732
  212.4 4.9 %copy-start.17 = (f32[3,18,1,128]{3,2,1,0:T(1,128)S(1)}, f32[3,18,1,128]{3,2,1,0:T(1,128)}, u32[]{:S(2)}) copy-start(f32[3,18,1,128]{3,2,1,0:T(1,128)} %copy-done.16) | copy-start | bytes 82948
  212.4 4.9 %copy-start.21 = (f32[3,18,1,128]{3,2,1,0:T(1,128)S(1)}, f32[3,18,1,128]{3,2,1,0:T(1,128)}, u32[]{:S(2)}) copy-start(f32[3,18,1,128]{3,2,1,0:T(1,128)} %copy-done.20) | copy-start | bytes 82948
  (5 other events, 4.3 us)
where the time goes:
time: 220 us; the launch traced here: 219 us
  starting transfers between devices  84.3 us (38%)
  local copies, waits for them, and re-layouts  73.3 us (33%)
  waiting for transfers between devices  34 us (15%)
  other arithmetic  16 us (7%)
  matrix products  9.65 us (4%)
    ppermute x12, starting transfers between devices, extended(): before = lax.ppermute(last, axis, up)  44.7 us
    ppermute x12, waiting for transfers between devices, extended(): before = lax.ppermute(last, axis, up)  34 us
    ppermute x12, starting transfers between devices, extended(): after = lax.ppermute(leading, axis, down)  27.6 us
    slice x5, local copies, waits for them, and re-layouts, per_device(): u_next = 2.0 * u_now - u_prev + rate[None] * laplace + drive_all[step]  24.7 us
    all_to_all x1, starting transfers between devices, per_device(): lax.all_to_all(outgoing, 'gy', split_axis=0, concat_axis=0, tiled=True)  12.1 us
    squeeze x4, local copies, waits for them, and re-layouts, per_device(): u_next = 2.0 * u_now - u_prev + rate[None] * laplace + drive_all[step]  11.7 us
    slice x9, local copies, waits for them, and re-layouts, extended(): leading = lax.slice_in_dim(shard, 0, width, axis=dim)  11.5 us
    add x4, other arithmetic, per_device(): u_next = 2.0 * u_now - u_prev + rate[None] * laplace + drive_all[step]  11 us
  transfers between devices with their start and end apart: 25, of which 7 were waited for; matrix products, arithmetic and copies ran while one was open for 19% of the time, Pallas kernels for 0%

commit v1 on v0

v1 whole, which is shorter than its diff:
```python
import functools

import jax
import jax.numpy as jnp
import ml_dtypes
import numpy as np
from jax import lax
from jax.experimental import pallas as pl
from jax.experimental.pallas import tpu as pltpu
from jax.sharding import PartitionSpec as P

NSTEP = 4
MESH = pl.DeviceIdType.MESH
F32 = jnp.float32
BF16 = jnp.bfloat16


def wave_table(count):
    half = count // 2
    freq = np.float32(2.0 * np.pi) * (np.arange(half, dtype=np.float32) + np.float32(0.5)) / np.float32(count)
    times = np.float32(37.0) + np.arange(NSTEP, dtype=np.float32)
    phase = (freq[:, None] * times[None, :]).astype(np.float32)
    table = np.concatenate([np.cos(phase), np.sin(phase)], axis=0) / np.sqrt(np.float32(half))
    table = np.pad(table.T, ((0, 8 - NSTEP), (0, 0)))
    return table.astype(ml_dtypes.bfloat16)


def split_dot(a, b, dims):
    hi = b.astype(BF16)
    lo = (b - hi.astype(F32)).astype(BF16)
    one = a.astype(BF16)
    return lax.dot_general(one, hi, (dims, ((), ())), preferred_element_type=F32) + lax.dot_general(
        one, lo, (dims, ((), ())), preferred_element_type=F32
    )


def kernel(
    n_gx, n_gy, u_hbm, up_hbm, pan_hbm, own_hbm, blk_hbm, cpl_hbm, dep_hbm, spd_hbm, lat_hbm, tab_hbm,
    out_now, out_prev,
    U, up, pan, own, blk, cpl, dep, spd, lat, tab, G, W, D, msend, mrecv,
    ysend, yrecv, zsend, zrecv,
    in_sem, fsend_sem, frecv_sem, x_send, x_recv, y_send, y_recv, z_send, z_recv,
):
    gx, gy, gz = lax.axis_index("gx"), lax.axis_index("gy"), lax.axis_index("gz")
    loads = [
        pltpu.make_async_copy(pan_hbm, pan, in_sem.at[0]),
        pltpu.make_async_copy(tab_hbm, tab, in_sem.at[1]),
        pltpu.make_async_copy(own_hbm, own, in_sem.at[2]),
        pltpu.make_async_copy(blk_hbm, blk, in_sem.at[3]),
        pltpu.make_async_copy(cpl_hbm, cpl, in_sem.at[4]),
        pltpu.make_async_copy(u_hbm, U.at[0, :, 1:17], in_sem.at[5]),
        pltpu.make_async_copy(up_hbm, up, in_sem.at[6]),
        pltpu.make_async_copy(lat_hbm, lat, in_sem.at[7]),
        pltpu.make_async_copy(dep_hbm, dep, in_sem.at[8]),
        pltpu.make_async_copy(spd_hbm, spd, in_sem.at[9]),
    ]
    for copy in loads:
        copy.start()

    barrier = pltpu.get_barrier_semaphore()

    @pl.loop(1, n_gy)
    def _(k):
        pl.semaphore_signal(barrier, inc=1, device_id={"gy": lax.rem(gy + k, n_gy)}, device_id_type=MESH)

    pl.semaphore_signal(barrier, inc=1, device_id={"gz": 1 - gz}, device_id_type=MESH)
    has_left, has_right = gx > 0, gx < n_gx - 1
    has_down, has_up = gy > 0, gy < n_gy - 1

    @pl.when(has_left)
    def _():
        pl.semaphore_signal(barrier, inc=1, device_id={"gx": gx - 1}, device_id_type=MESH)

    @pl.when(has_right)
    def _():
        pl.semaphore_signal(barrier, inc=1, device_id={"gx": gx + 1}, device_id_type=MESH)

    @pl.when(jnp.logical_not(has_left))
    def _():
        U[:, :, 0] = jnp.zeros((NSTEP, 3, 16, 128), F32)

    @pl.when(jnp.logical_not(has_right))
    def _():
        U[:, :, 17] = jnp.zeros((NSTEP, 3, 16, 128), F32)

    @pl.when(jnp.logical_not(has_down))
    def _():
        yrecv[:, 0] = jnp.zeros((NSTEP, 3, 16, 128), F32)

    @pl.when(jnp.logical_not(has_up))
    def _():
        yrecv[:, 1] = jnp.zeros((NSTEP, 3, 16, 128), F32)

    edge = 127 - 127 * gz
    lane16 = lax.broadcasted_iota(jnp.int32, (16, 128), 1)
    row16 = lax.broadcasted_iota(jnp.int32, (16, 128), 0)

    for copy in loads[2:4]:
        copy.wait()
    owner = own[...]
    q = lax.broadcasted_iota(jnp.int32, (1, 384), 1)
    rank = jnp.zeros((1, 384), jnp.int32)
    for d in range(1, 16):
        same = jnp.logical_and(q % 16 >= d, pltpu.roll(owner, d, 1) == owner)
        rank = rank + same.astype(jnp.int32)
    own[...] = owner + 64 * rank
    code = own[...]
    k48 = lax.broadcasted_iota(jnp.int32, (48, 384), 0)
    q48 = lax.broadcasted_iota(jnp.int32, (48, 384), 1)
    slot, src = k48 // 24, k48 % 24
    mine = jnp.logical_and(code == gy + 64 * slot, q48 // 16 == src)
    slot_block = jnp.sum(jnp.where(mine, blk[...] + 1, 0), axis=1, keepdims=True) - 1

    tile = gy // 8
    off = (gy - 8 * tile) * 16
    lane1 = lax.broadcasted_iota(jnp.int32, (1, 128), 1)
    mycode = own[:, pl.ds(pl.multiple_of(tile * 128, 128), 128)]
    mycode = jnp.where(jnp.logical_and(lane1 >= off, lane1 < off + 16), mycode, 0)
    for s in (16, 32, 64):
        mycode = mycode + pltpu.roll(mycode, s, 1)
    r192 = lax.broadcasted_iota(jnp.int32, (192, 128), 0)
    l192 = lax.broadcasted_iota(jnp.int32, (192, 128), 1)
    want = (r192 % 24) + 64 * (r192 // 96)
    step_of = (r192 // 24) % 4
    pick = jnp.where(jnp.logical_and(mycode == want, l192 // 16 == step_of), 1.0, 0.0)

    for copy in loads[:2]:
        copy.wait()
    free = lax.dot_general(tab[...], pan[...], (((1,), (1,)), ((), ())), preferred_element_type=F32)
    G[...] = jnp.zeros_like(G)
    for p in range(16):
        G[:, p, :48] = free[:, 48 * p : 48 * p + 48]
    loads[4].wait()
    zero = jnp.zeros((16, 16), F32)
    stiff = jnp.concatenate(
        [jnp.concatenate([cpl[c] if c == k else zero for k in range(3)], axis=1) for c in range(3)], axis=0
    )
    force = lax.dot_general(
        G[...].reshape(128, 128)[:, :48], stiff, (((1,), (1,)), ((), ())),
        precision=lax.Precision.HIGHEST, preferred_element_type=F32,
    )
    picked = split_dot(pick, force, ((1,), (0,)))
    picked = jnp.concatenate([picked, jnp.zeros((192, 80), F32)], axis=1)
    lane24 = lax.broadcasted_iota(jnp.int32, (24, 128), 1)
    for c in range(3):
        message = jnp.zeros((24, 128), F32)
        for sn in range(8):
            part = picked[24 * sn : 24 * sn + 24]
            shift = (16 * (sn - c)) % 128
            if shift:
                part = pltpu.roll(part, shift, 1)
            message = jnp.where(lane24 // 16 == sn, part, message)
        msend[:, c, :] = message
    mrecv[gy] = msend[gy]

    near = 1 + has_left.astype(jnp.int32) + has_right.astype(jnp.int32)
    pl.semaphore_wait(barrier, n_gy - 1 + near)

    def message_copy(peer, sender):
        return pltpu.make_async_remote_copy(
            src_ref=msend.at[peer], dst_ref=mrecv.at[sender], send_sem=fsend_sem.at[peer],
            recv_sem=frecv_sem.at[sender], device_id={"gy": peer}, device_id_type=MESH,
        )

    @pl.loop(1, n_gy)
    def _(k):
        message_copy(lax.rem(gy + k, n_gy), gy).start()

    def x_copy(step, side):
        return pltpu.make_async_remote_copy(
            src_ref=U.at[step, :, 1 + 15 * side], dst_ref=U.at[step, :, 17 - 17 * side],
            send_sem=x_send.at[step, side], recv_sem=x_recv.at[step, side],
            device_id={"gx": gx - 1 + 2 * side}, device_id_type=MESH,
        )

    def y_copy(step, side):
        return pltpu.make_async_remote_copy(
            src_ref=ysend.at[step, side], dst_ref=yrecv.at[step, 1 - side],
            send_sem=y_send.at[step, side], recv_sem=y_recv.at[step, side],
            device_id={"gy": gy - 1 + 2 * side}, device_id_type=MESH,
        )

    def z_copy(step):
        return pltpu.make_async_remote_copy(
            src_ref=zsend.at[step], dst_ref=zrecv.at[step], send_sem=z_send.at[step], recv_sem=z_recv.at[step],
            device_id={"gz": 1 - gz}, device_id_type=MESH,
        )

    def start_faces(step):
        for side, there in ((0, has_left), (1, has_right)):
            pl.when(there)(lambda side=side: x_copy(step, side).start())
        for side, there in ((0, has_down), (1, has_up)):
            pl.when(there)(lambda side=side: y_copy(step, side).start())
        z_copy(step).start()

    def wait_faces(step):
        for side, there in ((0, has_right), (1, has_left)):
            pl.when(there)(lambda side=side: x_copy(step, side).wait_recv())
        for side, there in ((0, has_up), (1, has_down)):
            pl.when(there)(lambda side=side: y_copy(step, side).wait_recv())
        z_copy(step).wait_recv()

    def wait_sent(step):
        for side, there in ((0, has_left), (1, has_right)):
            pl.when(there)(lambda side=side: x_copy(step, side).wait_send())
        for side, there in ((0, has_down), (1, has_up)):
            pl.when(there)(lambda side=side: y_copy(step, side).wait_send())
        z_copy(step).wait_send()

    def pack(step, x, c, value, packed):
        ysend[step, 0, c, pl.ds(x, 1), :] = value[0:1]
        ysend[step, 1, c, pl.ds(x, 1), :] = value[15:16]
        place = 16 * c + x
        turned = pltpu.roll(value, lax.rem(place - edge + 128, 128), 1)
        return jnp.where(lane16 == place, turned, packed)

    loads[5].wait()

    def pack_first(x, packed):
        for c in range(3):
            packed = pack(0, x, c, U[0, c, x + 1], packed)
        return packed

    zsend[0] = lax.fori_loop(0, 16, pack_first, jnp.zeros((16, 128), F32))
    start_faces(0)

    for copy in loads[6:]:
        copy.wait()
    speed = jnp.zeros((1, 128), F32)
    for layer in range(spd.shape[1]):
        speed = jnp.where(dep[...] == layer, spd[0:1, layer : layer + 1], speed)
    lat[...] = lat[...] * speed[None]

    @pl.loop(1, n_gy)
    def _(k):
        peer = lax.rem(gy + n_gy - k, n_gy)
        message_copy(peer, peer).wait_recv()

    for s in range(2):
        block_s = slot_block[24 * s : 24 * s + 24]
        zb = jnp.bitwise_and(block_s, 7)
        for c in range(3):
            row = mrecv[:, c, :]
            for b in range(3):
                row = jnp.where(jnp.bitwise_and(zb, 1 << b) > 0, pltpu.roll(row, 16 << b, 1), row)
            for n in range(NSTEP):
                shift = (-16 * (4 * s + n)) % 128
                moved = pltpu.roll(row, shift, 1) if shift else row
                at = (3 * n + c) * 128
                W[24 * s : 24 * s + 24, at : at + 128] = jnp.where(lane24 // 16 == zb, moved, 0.0)
    column = lax.shift_right_arithmetic(slot_block, 3)
    onehot = jnp.where(column == lax.broadcasted_iota(jnp.int32, (48, 256), 1), 1.0, 0.0)
    D[...] = split_dot(onehot, W[...], ((0,), (0,)))

    for step in range(NSTEP):
        wait_faces(step)
        halo_z = zrecv[step]

        def advance(x, packed, step=step):
            rate = lat[x]
            for c in range(3):
                v = U[step, c, x + 1]
                below = jnp.where(row16 == 0, yrecv[step, 0, c, pl.ds(x, 1), :], pltpu.roll(v, 1, 0))
                above = jnp.where(row16 == 15, yrecv[step, 1, c, pl.ds(x, 1), :], pltpu.roll(v, 15, 0))
                turned = pltpu.roll(halo_z, lax.rem(edge - (16 * c + x) + 128, 128), 1)
                halo = jnp.where(lane16 == edge, turned, 0.0)
                z0 = jnp.where(lane16 == 0, 0.0, pltpu.roll(v, 1, 1))
                z1 = jnp.where(lane16 == 127, 0.0, pltpu.roll(v, 127, 1))
                around = U[step, c, x] + U[step, c, x + 2] + below + above + (z0 + z1 + halo)
                old = up[c, x] if step == 0 else U[step - 1, c, x + 1]
                at = (3 * step + c) * 128
                drive = D[pl.ds(pl.multiple_of(16 * x, 16), 16), at : at + 128]
                new = (2.0 * v - old) + rate * (around - 6.0 * v) + drive
                if step < NSTEP - 1:
                    U[step + 1, c, x + 1] = new
                    packed = pack(step + 1, x, c, new, packed)
                else:
                    out_now[c, x] = new
                    out_prev[c, x] = v
            return packed

        packed = lax.fori_loop(0, 16, advance, jnp.zeros((16, 128), F32))
        if step < NSTEP - 1:
            zsend[step + 1] = packed
            start_faces(step + 1)

    for step in range(NSTEP):
        wait_sent(step)

    @pl.loop(1, n_gy)
    def _(k):
        message_copy(lax.rem(gy + k, n_gy), gy).wait_send()


def per_device(n_gx, n_gy, u_now, u_prev, panels, panel_owner, panel_block, coupling, layer_depth, layer_speed, lateral):
    spectral = panels.shape[4]
    count = panel_owner.shape[2]
    layers = layer_speed.shape[0]
    table = jnp.asarray(wave_table(spectral))
    anywhere = pl.BlockSpec(memory_space=pl.ANY)
    vmem = pl.BlockSpec(memory_space=pltpu.VMEM)
    dma = pltpu.SemaphoreType.DMA
    return pl.pallas_call(
        functools.partial(kernel, n_gx, n_gy),
        out_shape=(jax.ShapeDtypeStruct(u_now.shape, F32), jax.ShapeDtypeStruct(u_now.shape, F32)),
        in_specs=[anywhere] * 10,
        out_specs=(vmem, vmem),
        scratch_shapes=[
            pltpu.VMEM((NSTEP, 3, 18, 16, 128), F32),
            pltpu.VMEM(u_prev.shape, F32),
            pltpu.VMEM((768, spectral), BF16),
            pltpu.VMEM((1, count), jnp.int32),
            pltpu.VMEM((1, count), jnp.int32),
            pltpu.VMEM(coupling.shape, F32),
            pltpu.VMEM((1, 128), jnp.int32),
            pltpu.VMEM((1, layers), F32),
            pltpu.VMEM(lateral.shape, F32),
            pltpu.VMEM(table.shape, BF16),
            pltpu.VMEM((8, 16, 128), F32),
            pltpu.VMEM((48, 1536), F32),
            pltpu.VMEM((256, 1536), F32),
            pltpu.VMEM((24, 3, 128), F32),
            pltpu.VMEM((24, 3, 128), F32),
            pltpu.VMEM((NSTEP, 2, 3, 16, 128), F32),
            pltpu.VMEM((NSTEP, 2, 3, 16, 128), F32),
            pltpu.VMEM((NSTEP, 16, 128), F32),
            pltpu.VMEM((NSTEP, 16, 128), F32),
            dma((10,)),
            dma((24,)),
            dma((24,)),
            dma((NSTEP, 2)),
            dma((NSTEP, 2)),
            dma((NSTEP, 2)),
            dma((NSTEP, 2)),
            dma((NSTEP,)),
            dma((NSTEP,)),
        ],
        compiler_params=pltpu.CompilerParams(collective_id=0, has_side_effects=True),
        name="domain_reduction",
    )(
        u_now, u_prev, panels.reshape(768, spectral), panel_owner.reshape(1, count), panel_block.reshape(1, count),
        coupling, layer_depth.reshape(1, 128), layer_speed.reshape(1, layers), lateral, table,
    )


def solution(mesh):
    in_specs = (
        P(None, "gx", "gy", "gz"),
        P(None, "gx", "gy", "gz"),
        P("gx", "gz", "gy", None, None),
        P("gx", "gz", None, None),
        P("gx", "gz", None),
        P(),
        P("gz"),
        P(),
        P("gx", "gy", "gz"),
    )
    out_specs = (P(None, "gx", "gy", "gz"), P(None, "gx", "gy", "gz"))
    return jax.shard_map(
        functools.partial(per_device, mesh.shape["gx"], mesh.shape["gy"]),
        mesh=mesh, in_specs=in_specs, out_specs=out_specs, check_vma=False,
    )
```

time: 220 us -> 52.8 us (0.24)
  the two profiles are of different devices: /device:TPU:260 before, /device:TPU:6 now
where the time goes in v1:
time: 52.8 us; the launch traced here: 52.6 us
  Pallas kernels  49.4 us (94%)
  local copies, waits for them, and re-layouts  2.57 us (5%)
  between operations  0.65 us (1%)
    pallas_call x1, Pallas kernels, per_device(): pl.pallas_call(functools.partial(kernel, n_gx, n_gy), out_shape=(jax.Shap...  49.4 us
    unnamed x4, local copies, waits for them, and re-layouts  2.57 us

profile of v1, /device:TPU:6, one launch (start us, length us, event | category | flops | bytes accessed | tf_op | source)
XLA Modules:
  0.0 52.6 jit_solution(2665934691662773016)
XLA Ops:
  0.6 49.4 %domain_reduction.1 = (f32[3,16,16,128]{3,2,1,0:T(8,128)}, f32[3,16,16,128]{3,2,1,0:T(8,128)}) custom-call(f32[3,16,16,128]{3,2,1,0:T(8,128)} %u_hbm.1, f32[3,16,16,128]{3,2,1,0:T(8,128)} %up_hbm.1, bf16[768,256]{1,0:T(8,128)(2,1)} %bitcast.5, s32[1,384]{1,0:T(1,128)} %bitcast.6, s32[1,384]{1,0:T(1,128)} %bitcast.7, f32[3,16,16]{2,1,0:T(8,128)} %cpl_hbm.1, ...), custom_call_target="tpu_custom_call" | custom-call | tf_op jit(solution)/shard_map/domain_reduction/pallas_call | solution.py:303
  50.0 0.0 copy-start
  50.0 1.8 %copy.14 = f32[3,16,16,128]{3,2,1,0:T(8,128)} copy(f32[3,16,16,128]{3,2,1,0:T(8,128)} %get-tuple-element.4) | data formatting | bytes 786432
  51.8 0.0 copy-done
  51.8 0.7 %copy.15 = f32[3,16,16,128]{3,2,1,0:T(8,128)} copy(f32[3,16,16,128]{3,2,1,0:T(8,128)S(1)} %copy-done) | data formatting | bytes 786432
Async XLA Ops:
  50.0 1.8 %copy-start = (f32[3,16,16,128]{3,2,1,0:T(8,128)S(1)}, f32[3,16,16,128]{3,2,1,0:T(8,128)}, u32[]{:S(2)}) copy-start(f32[3,16,16,128]{3,2,1,0:T(8,128)} %get-tuple-element.5) | copy-start | bytes 1179652

commit v2 on v1

v2 whole, which is shorter than its diff:
```python
import functools

import jax
import jax.numpy as jnp
import ml_dtypes
import numpy as np
from jax import lax
from jax.experimental import pallas as pl
from jax.experimental.pallas import tpu as pltpu
from jax.sharding import PartitionSpec as P

NSTEP = 4
MESH = pl.DeviceIdType.MESH
F32 = jnp.float32
BF16 = jnp.bfloat16


def wave_table(count):
    half = count // 2
    freq = np.float32(2.0 * np.pi) * (np.arange(half, dtype=np.float32) + np.float32(0.5)) / np.float32(count)
    times = np.float32(37.0) + np.arange(NSTEP, dtype=np.float32)
    phase = (freq[:, None] * times[None, :]).astype(np.float32)
    table = np.concatenate([np.cos(phase), np.sin(phase)], axis=0) / np.sqrt(np.float32(half))
    table = np.pad(table.T, ((0, 8 - NSTEP), (0, 0)))
    return table.astype(ml_dtypes.bfloat16)


def two_parts(b):
    hi = b.astype(BF16)
    lo = (b - hi.astype(F32)).astype(BF16)
    return jnp.concatenate([hi, lo], axis=0)


def kernel(
    n_gx, n_gy, u_hbm, up_hbm, pan_hbm, own_hbm, blk_hbm, cpl_hbm, dep_hbm, spd_hbm, lat_hbm, tab_hbm,
    out_now, out_prev,
    U, up, pan, own, blk, cpl, dep, spd, lat, tab, G, D, msend, mrecv, zsend, zrecv,
    in_sem, fsend_sem, frecv_sem, x_send, x_recv, y_send, y_recv, z_send, z_recv,
):
    gx, gy, gz = lax.axis_index("gx"), lax.axis_index("gy"), lax.axis_index("gz")
    loads = [
        pltpu.make_async_copy(pan_hbm, pan, in_sem.at[0]),
        pltpu.make_async_copy(tab_hbm, tab, in_sem.at[1]),
        pltpu.make_async_copy(own_hbm, own, in_sem.at[2]),
        pltpu.make_async_copy(blk_hbm, blk, in_sem.at[3]),
        pltpu.make_async_copy(cpl_hbm, cpl, in_sem.at[4]),
        pltpu.make_async_copy(u_hbm, U.at[0, :, 1:17, 8:24], in_sem.at[5]),
        pltpu.make_async_copy(up_hbm, up, in_sem.at[6]),
        pltpu.make_async_copy(lat_hbm, lat, in_sem.at[7]),
        pltpu.make_async_copy(dep_hbm, dep, in_sem.at[8]),
        pltpu.make_async_copy(spd_hbm, spd, in_sem.at[9]),
    ]
    for at in (2, 0, 1, 3, 4, 5, 6, 7, 8, 9):
        loads[at].start()

    barrier = pltpu.get_barrier_semaphore()

    @pl.loop(1, n_gy)
    def _(k):
        pl.semaphore_signal(barrier, inc=1, device_id={"gy": lax.rem(gy + k, n_gy)}, device_id_type=MESH)

    pl.semaphore_signal(barrier, inc=1, device_id={"gz": 1 - gz}, device_id_type=MESH)
    has_left, has_right = gx > 0, gx < n_gx - 1
    has_down, has_up = gy > 0, gy < n_gy - 1

    @pl.when(has_left)
    def _():
        pl.semaphore_signal(barrier, inc=1, device_id={"gx": gx - 1}, device_id_type=MESH)

    @pl.when(has_right)
    def _():
        pl.semaphore_signal(barrier, inc=1, device_id={"gx": gx + 1}, device_id_type=MESH)

    @pl.when(jnp.logical_not(has_left))
    def _():
        U[:, :, 0, 8:24] = jnp.zeros((NSTEP, 3, 16, 128), F32)

    @pl.when(jnp.logical_not(has_right))
    def _():
        U[:, :, 17, 8:24] = jnp.zeros((NSTEP, 3, 16, 128), F32)

    @pl.when(jnp.logical_not(has_down))
    def _():
        U[:, :, 1:17, 0:8] = jnp.zeros((NSTEP, 3, 16, 8, 128), F32)

    @pl.when(jnp.logical_not(has_up))
    def _():
        U[:, :, 1:17, 24:32] = jnp.zeros((NSTEP, 3, 16, 8, 128), F32)

    edge = 127 - 127 * gz
    lane16 = lax.broadcasted_iota(jnp.int32, (16, 128), 1)
    at_edge = lane16 == edge
    at_low, at_high = lane16 == 0, lane16 == 127

    loads[2].wait()
    owner = own[...]
    q = lax.broadcasted_iota(jnp.int32, (1, 384), 1)
    rank = jnp.zeros((1, 384), jnp.int32)
    for d in range(1, 16):
        same = jnp.logical_and(q % 16 >= d, pltpu.roll(owner, d, 1) == owner)
        rank = rank + same.astype(jnp.int32)
    own[...] = owner + 64 * rank

    tile = gy // 8
    off = (gy - 8 * tile) * 16
    lane1 = lax.broadcasted_iota(jnp.int32, (1, 128), 1)
    mycode = own[:, pl.ds(pl.multiple_of(tile * 128, 128), 128)]
    mycode = jnp.where(jnp.logical_and(lane1 >= off, lane1 < off + 16), mycode, 0)
    for s in (16, 32, 64):
        mycode = mycode + pltpu.roll(mycode, s, 1)
    r192 = lax.broadcasted_iota(jnp.int32, (192, 128), 0)
    l192 = lax.broadcasted_iota(jnp.int32, (192, 128), 1)
    want = (r192 % 24) + 64 * (r192 // 96)
    step_of = (r192 // 24) % 4
    pick = jnp.where(jnp.logical_and(mycode == want, l192 // 16 == step_of), 1.0, 0.0).astype(BF16)
    pick = jnp.concatenate([pick, pick], axis=1)

    G[...] = jnp.zeros_like(G)
    loads[4].wait()
    zero = jnp.zeros((16, 16), F32)
    stiff = jnp.concatenate(
        [jnp.concatenate([cpl[c] if c == k else zero for k in range(3)], axis=1) for c in range(3)], axis=0
    )
    loads[0].wait()
    loads[1].wait()
    free = lax.dot_general(tab[...], pan[...], (((1,), (1,)), ((), ())), preferred_element_type=F32)
    for p in range(16):
        G[:, p, :48] = free[:, 48 * p : 48 * p + 48]
    force = lax.dot_general(
        G[...].reshape(128, 128)[:, :48], stiff, (((1,), (1,)), ((), ())),
        precision=lax.Precision.HIGHEST, preferred_element_type=F32,
    )
    picked = jnp.dot(pick, two_parts(force), preferred_element_type=F32)
    picked = jnp.concatenate([picked, jnp.zeros((192, 80), F32)], axis=1)
    lane24 = lax.broadcasted_iota(jnp.int32, (24, 128), 1)
    for c in range(3):
        message = jnp.zeros((24, 128), F32)
        for sn in range(8):
            part = picked[24 * sn : 24 * sn + 24]
            shift = (16 * (sn - c)) % 128
            if shift:
                part = pltpu.roll(part, shift, 1)
            message = jnp.where(lane24 // 16 == sn, part, message)
        msend[:, c, :] = message
    mrecv[gy] = msend[gy]

    near = 1 + has_left.astype(jnp.int32) + has_right.astype(jnp.int32)
    loads[5].wait()
    pl.semaphore_wait(barrier, n_gy - 1 + near)

    def message_copy(peer, sender):
        return pltpu.make_async_remote_copy(
            src_ref=msend.at[peer], dst_ref=mrecv.at[sender], send_sem=fsend_sem.at[peer],
            recv_sem=frecv_sem.at[sender], device_id={"gy": peer}, device_id_type=MESH,
        )

    def x_copy(step, side):
        return pltpu.make_async_remote_copy(
            src_ref=U.at[step, :, 1 + 15 * side, 8:24], dst_ref=U.at[step, :, 17 - 17 * side, 8:24],
            send_sem=x_send.at[step, side], recv_sem=x_recv.at[step, side],
            device_id={"gx": gx - 1 + 2 * side}, device_id_type=MESH,
        )

    def y_copy(step, side):
        here, there = 8 + 15 * side, 24 - 17 * side
        return pltpu.make_async_remote_copy(
            src_ref=U.at[step, :, 1:17, here : here + 1], dst_ref=U.at[step, :, 1:17, there : there + 1],
            send_sem=y_send.at[step, side], recv_sem=y_recv.at[step, side],
            device_id={"gy": gy - 1 + 2 * side}, device_id_type=MESH,
        )

    def z_copy(step):
        return pltpu.make_async_remote_copy(
            src_ref=zsend.at[step], dst_ref=zrecv.at[step], send_sem=z_send.at[step], recv_sem=z_recv.at[step],
            device_id={"gz": 1 - gz}, device_id_type=MESH,
        )

    def start_x(step):
        for side, there in ((0, has_left), (1, has_right)):
            pl.when(there)(lambda side=side: x_copy(step, side).start())

    def start_yz(step):
        for side, there in ((0, has_down), (1, has_up)):
            pl.when(there)(lambda side=side: y_copy(step, side).start())
        z_copy(step).start()

    def wait_faces(step):
        for side, there in ((0, has_up), (1, has_down)):
            pl.when(there)(lambda side=side: y_copy(step, side).wait_recv())
        z_copy(step).wait_recv()
        for side, there in ((0, has_right), (1, has_left)):
            pl.when(there)(lambda side=side: x_copy(step, side).wait_recv())

    def wait_sent(step):
        for side, there in ((0, has_left), (1, has_right)):
            pl.when(there)(lambda side=side: x_copy(step, side).wait_send())
        for side, there in ((0, has_down), (1, has_up)):
            pl.when(there)(lambda side=side: y_copy(step, side).wait_send())
        z_copy(step).wait_send()

    def pack(place, value, packed):
        turned = pltpu.roll(value, place, 1) if place else value
        return jnp.where(lane16 == jnp.bitwise_and(edge + place, 127), turned, packed)

    start_x(0)

    @pl.loop(1, n_gy)
    def _(k):
        message_copy(lax.rem(gy + k, n_gy), gy).start()

    packed = jnp.zeros((16, 128), F32)
    for c in range(3):
        for x in range(16):
            packed = pack(16 * c + x, U[0, c, x + 1, 8:24], packed)
    zsend[0] = packed
    start_yz(0)

    loads[3].wait()
    k48 = lax.broadcasted_iota(jnp.int32, (48, 384), 0)
    q48 = lax.broadcasted_iota(jnp.int32, (48, 384), 1)
    late = k48 >= 32
    slot = jnp.where(late, (k48 - 32) // 8, k48 // 16)
    src = jnp.where(late, 16 + k48 % 8, k48 % 16)
    mine = jnp.logical_and(own[...] == gy + 64 * slot, q48 // 16 == src)
    slot_block = jnp.sum(jnp.where(mine, blk[...] + 1, 0), axis=1, keepdims=True) - 1
    column = lax.shift_right_arithmetic(slot_block, 3)
    hot = jnp.where(column == lax.broadcasted_iota(jnp.int32, (48, 256), 1), 1.0, 0.0)
    hot = jnp.transpose(jnp.concatenate([hot, jnp.zeros((80, 256), F32)], axis=0)).astype(BF16)
    hot_early = jnp.concatenate([hot[:, :32], hot[:, :32]], axis=1)
    hot_late = jnp.concatenate([hot[:, 32:48], hot[:, 32:48]], axis=1)

    for copy in loads[6:]:
        copy.wait()
    speed = jnp.zeros((1, 128), F32)
    for layer in range(spd.shape[1]):
        speed = jnp.where(dep[...] == layer, spd[0:1, layer : layer + 1], speed)
    lat[...] = lat[...] * speed[None]

    def turned_rows(first, count, at):
        out = []
        for s in range(2):
            zb = jnp.bitwise_and(slot_block[at + count * s : at + count * (s + 1)], 7)
            for c in range(3):
                row = mrecv[first : first + count, c, :]
                for b in range(3):
                    row = jnp.where(jnp.bitwise_and(zb, 1 << b) > 0, pltpu.roll(row, 16 << b, 1), row)
                out.append((s, c, zb, row))
        return out

    def placed(rows, count, hot, n):
        lanes = lax.broadcasted_iota(jnp.int32, (count, 128), 1) // 16
        parts = [[], []]
        for s, c, zb, row in rows:
            shift = (-16 * (4 * s + n)) % 128
            moved = pltpu.roll(row, shift, 1) if shift else row
            parts[s].append(jnp.where(lanes == zb, moved, 0.0))
        w = jnp.concatenate([jnp.concatenate(part, axis=1) for part in parts], axis=0)
        return jnp.dot(hot, two_parts(w), preferred_element_type=F32)

    def stencil(step, c, x, halo):
        v = U[step, c, x + 1, 8:24]
        place = 16 * c + x
        turned = pltpu.roll(halo, (128 - place) % 128, 1) if place else halo
        z = (
            jnp.where(at_low, 0.0, pltpu.roll(v, 1, 1))
            + jnp.where(at_high, 0.0, pltpu.roll(v, 127, 1))
            + jnp.where(at_edge, turned, 0.0)
        )
        y = U[step, c, x + 1, 7:23] + U[step, c, x + 1, 9:25]
        around = (U[step, c, x, 8:24] + U[step, c, x + 2, 8:24]) + y + z
        old = up[c, x] if step == 0 else U[step - 1, c, x + 1, 8:24]
        return (2.0 * v - old) + lat[x] * (around - 6.0 * v)

    order = [0, 15] + list(range(1, 15))

    def halo_of(step):
        return pltpu.roll(zrecv[step], jnp.bitwise_and(127 + 2 * gz, 127), 1)

    wait_faces(0)
    halo = halo_of(0)
    for x in order:
        for c in range(3):
            U[1, c, x + 1, 8:24] = stencil(0, c, x, halo)

    def message_wait(peer):
        pl.when(peer != gy)(lambda: message_copy(peer, peer).wait_recv())

    pl.loop(0, 16)(message_wait)
    rows = turned_rows(0, 16, 0)
    for n in range(NSTEP):
        D[n] = placed(rows, 16, hot_early, n)
    pl.loop(16, 24)(message_wait)
    rows = turned_rows(16, 8, 32)
    drive = D[0] + placed(rows, 8, hot_late, 0)
    packed = jnp.zeros((16, 128), F32)
    for x in order:
        for c in range(3):
            new = U[1, c, x + 1, 8:24] + drive[16 * x : 16 * x + 16, 128 * c : 128 * c + 128]
            U[1, c, x + 1, 8:24] = new
            packed = pack(16 * c + x, new, packed)
        if x == 15:
            start_x(1)
    zsend[1] = packed
    start_yz(1)
    for n in range(1, NSTEP):
        D[n] = D[n] + placed(rows, 8, hot_late, n)

    for step in range(1, NSTEP):
        wait_faces(step)
        halo = halo_of(step)
        packed = jnp.zeros((16, 128), F32)
        for x in order:
            for c in range(3):
                drive = D[step, 16 * x : 16 * x + 16, 128 * c : 128 * c + 128]
                new = stencil(step, c, x, halo) + drive
                if step < NSTEP - 1:
                    U[step + 1, c, x + 1, 8:24] = new
                    packed = pack(16 * c + x, new, packed)
                    if step == NSTEP - 2:
                        out_prev[c, x] = new
                else:
                    out_now[c, x] = new
            if step < NSTEP - 1 and x == 15:
                start_x(step + 1)
        if step < NSTEP - 1:
            zsend[step + 1] = packed
            start_yz(step + 1)

    for step in range(NSTEP):
        wait_sent(step)

    @pl.loop(1, n_gy)
    def _(k):
        message_copy(lax.rem(gy + k, n_gy), gy).wait_send()


def per_device(n_gx, n_gy, u_now, u_prev, panels, panel_owner, panel_block, coupling, layer_depth, layer_speed, lateral):
    spectral = panels.shape[4]
    count = panel_owner.shape[2]
    layers = layer_speed.shape[0]
    table = jnp.asarray(wave_table(spectral))
    anywhere = pl.BlockSpec(memory_space=pl.ANY)
    vmem = pl.BlockSpec(memory_space=pltpu.VMEM)
    dma = pltpu.SemaphoreType.DMA
    return pl.pallas_call(
        functools.partial(kernel, n_gx, n_gy),
        out_shape=(pltpu.VMEM(u_now.shape, F32), pltpu.VMEM(u_now.shape, F32)),
        in_specs=[anywhere] * 10,
        out_specs=(vmem, vmem),
        scratch_shapes=[
            pltpu.VMEM((NSTEP, 3, 18, 32, 128), F32),
            pltpu.VMEM(u_prev.shape, F32),
            pltpu.VMEM((768, spectral), BF16),
            pltpu.VMEM((1, count), jnp.int32),
            pltpu.VMEM((1, count), jnp.int32),
            pltpu.VMEM(coupling.shape, F32),
            pltpu.VMEM((1, 128), jnp.int32),
            pltpu.VMEM((1, layers), F32),
            pltpu.VMEM(lateral.shape, F32),
            pltpu.VMEM(table.shape, BF16),
            pltpu.VMEM((8, 16, 128), F32),
            pltpu.VMEM((NSTEP, 256, 384), F32),
            pltpu.VMEM((24, 3, 128), F32),
            pltpu.VMEM((24, 3, 128), F32),
            pltpu.VMEM((NSTEP, 16, 128), F32),
            pltpu.VMEM((NSTEP, 16, 128), F32),
            dma((10,)),
            dma((24,)),
            dma((24,)),
            dma((NSTEP, 2)),
            dma((NSTEP, 2)),
            dma((NSTEP, 2)),
            dma((NSTEP, 2)),
            dma((NSTEP,)),
            dma((NSTEP,)),
        ],
        compiler_params=pltpu.CompilerParams(collective_id=0, has_side_effects=True),
        name="domain_reduction",
    )(
        u_now, u_prev, panels.reshape(768, spectral), panel_owner.reshape(1, count), panel_block.reshape(1, count),
        coupling, layer_depth.reshape(1, 128), layer_speed.reshape(1, layers), lateral, table,
    )


def solution(mesh):
    in_specs = (
        P(None, "gx", "gy", "gz"),
        P(None, "gx", "gy", "gz"),
        P("gx", "gz", "gy", None, None),
        P("gx", "gz", None, None),
        P("gx", "gz", None),
        P(),
        P("gz"),
        P(),
        P("gx", "gy", "gz"),
    )
    out_specs = (P(None, "gx", "gy", "gz"), P(None, "gx", "gy", "gz"))
    return jax.shard_map(
        functools.partial(per_device, mesh.shape["gx"], mesh.shape["gy"]),
        mesh=mesh, in_specs=in_specs, out_specs=out_specs, check_vma=False,
    )
```

time: 52.8 us -> 43 us (0.81)
  Pallas kernels: 49.4 us -> 40.7 us
  local copies, waits for them, and re-layouts: 2.57 us -> 1.49 us
    pallas_call x1, Pallas kernels: 49.4 us -> 40.7 us  [per_device(): pl.pallas_call(functools.partial(kernel, n_gx, n_gy), out_shape=(pltpu.VM...]
    unnamed x4 -> x2, local copies, waits for them, and re-layouts: 2.57 us -> 1.49 us
where the time goes in v2:
time: 43 us; the launch traced here: 42.9 us
  Pallas kernels  40.7 us (95%)
  local copies, waits for them, and re-layouts  1.49 us (3%)
  between operations  0.64 us (1%)
    pallas_call x1, Pallas kernels, per_device(): pl.pallas_call(functools.partial(kernel, n_gx, n_gy), out_shape=(pltpu.VM...  40.7 us
    unnamed x2, local copies, waits for them, and re-layouts  1.49 us

profile of v2, /device:TPU:6, one launch (start us, length us, event | category | flops | bytes accessed | tf_op | source)
XLA Modules:
  0.0 42.9 jit_solution(8229932395678489450)
XLA Ops:
  0.6 40.7 %domain_reduction.1 = (f32[3,16,16,128]{3,2,1,0:T(8,128)S(1)}, f32[3,16,16,128]{3,2,1,0:T(8,128)S(1)}) custom-call(f32[3,16,16,128]{3,2,1,0:T(8,128)} %u_hbm.1, f32[3,16,16,128]{3,2,1,0:T(8,128)} %up_hbm.1, bf16[768,256]{1,0:T(8,128)(2,1)} %bitcast.5, s32[1,384]{1,0:T(1,128)} %bitcast.6, s32[1,384]{1,0:T(1,128)} %bitcast.7, f32[3,16,16]{2,1,0:T(8,128)} %cpl_hbm.1, ...), custom_call_target="tpu_custom_call" | custom-call | tf_op jit(solution)/shard_map/domain_reduction/pallas_call | solution.py:345
  41.4 0.7 %copy.14 = f32[3,16,16,128]{3,2,1,0:T(8,128)} copy(f32[3,16,16,128]{3,2,1,0:T(8,128)S(1)} %get-tuple-element.2) | data formatting | bytes 786432
  42.1 0.7 %copy.15 = f32[3,16,16,128]{3,2,1,0:T(8,128)} copy(f32[3,16,16,128]{3,2,1,0:T(8,128)S(1)} %get-tuple-element.3) | data formatting | bytes 786432

commit v3 on v2

--- a/solution.py
+++ b/solution.py
@@ -55,14 +55,15 @@
 
     barrier = pltpu.get_barrier_semaphore()
 
-    @pl.loop(1, n_gy)
-    def _(k):
-        pl.semaphore_signal(barrier, inc=1, device_id={"gy": lax.rem(gy + k, n_gy)}, device_id_type=MESH)
-
-    pl.semaphore_signal(barrier, inc=1, device_id={"gz": 1 - gz}, device_id_type=MESH)
     has_left, has_right = gx > 0, gx < n_gx - 1
     has_down, has_up = gy > 0, gy < n_gy - 1
 
+    pl.semaphore_signal(barrier, inc=1, device_id={"gz": 1 - gz}, device_id_type=MESH)
+
+    @pl.when(has_down)
+    def _():
+        pl.semaphore_signal(barrier, inc=1, device_id={"gy": gy - 1}, device_id_type=MESH)
+
     @pl.when(has_left)
     def _():
         pl.semaphore_signal(barrier, inc=1, device_id={"gx": gx - 1}, device_id_type=MESH)
@@ -70,6 +71,10 @@
     @pl.when(has_right)
     def _():
         pl.semaphore_signal(barrier, inc=1, device_id={"gx": gx + 1}, device_id_type=MESH)
+
+    @pl.loop(gy + 1, n_gy)
+    def _(peer):
+        pl.semaphore_signal(barrier, inc=1, device_id={"gy": peer}, device_id_type=MESH)
 
     @pl.when(jnp.logical_not(has_left))
     def _():
@@ -144,9 +149,9 @@
         msend[:, c, :] = message
     mrecv[gy] = msend[gy]
 
-    near = 1 + has_left.astype(jnp.int32) + has_right.astype(jnp.int32)
+    near = 1 + has_left.astype(jnp.int32) + has_right.astype(jnp.int32) + has_up.astype(jnp.int32)
     loads[5].wait()
-    pl.semaphore_wait(barrier, n_gy - 1 + near)
+    pl.semaphore_wait(barrier, gy + near)
 
     def message_copy(peer, sender):
         return pltpu.make_async_remote_copy(
@@ -204,9 +209,9 @@
 
     start_x(0)
 
-    @pl.loop(1, n_gy)
-    def _(k):
-        message_copy(lax.rem(gy + k, n_gy), gy).start()
+    @pl.loop(0, gy)
+    def _(peer):
+        message_copy(peer, gy).start()
 
     packed = jnp.zeros((16, 128), F32)
     for c in range(3):
@@ -283,13 +288,20 @@
             U[1, c, x + 1, 8:24] = stencil(0, c, x, halo)
 
     def message_wait(peer):
-        pl.when(peer != gy)(lambda: message_copy(peer, peer).wait_recv())
-
-    pl.loop(0, 16)(message_wait)
+        message_copy(peer, peer).wait_recv()
+
+    def message_reply(peer):
+        message_copy(peer, peer).wait_recv()
+        message_copy(peer, gy).start()
+
+    turn = jnp.where(gy < 16, 16, n_gy)
+    pl.loop(gy + 1, turn)(message_reply)
+    pl.loop(0, jnp.minimum(gy, 16))(message_wait)
     rows = turned_rows(0, 16, 0)
     for n in range(NSTEP):
         D[n] = placed(rows, 16, hot_early, n)
-    pl.loop(16, 24)(message_wait)
+    pl.loop(turn, n_gy)(message_reply)
+    pl.loop(16, gy)(message_wait)
     rows = turned_rows(16, 8, 32)
     drive = D[0] + placed(rows, 8, hot_late, 0)
     packed = jnp.zeros((16, 128), F32)

time: 43 us -> 40.6 us (0.944)
  the two profiles are of different devices: /device:TPU:6 before, /device:TPU:647 now
where the time goes in v3:
time: 40.6 us; the launch traced here: 40.5 us
  Pallas kernels  38.4 us (95%)
  local copies, waits for them, and re-layouts  1.49 us (4%)
  between operations  0.64 us (2%)
    pallas_call x1, Pallas kernels, per_device(): pl.pallas_call(functools.partial(kernel, n_gx, n_gy), out_shape=(pltpu.VM...  38.4 us
    unnamed x2, local copies, waits for them, and re-layouts  1.49 us

profile of v3, /device:TPU:647, one launch (start us, length us, event | category | flops | bytes accessed | tf_op | source)
XLA Modules:
  0.0 40.5 jit_solution(16062597472721137144)
XLA Ops:
  0.6 38.4 %domain_reduction.1 = (f32[3,16,16,128]{3,2,1,0:T(8,128)S(1)}, f32[3,16,16,128]{3,2,1,0:T(8,128)S(1)}) custom-call(f32[3,16,16,128]{3,2,1,0:T(8,128)} %u_hbm.1, f32[3,16,16,128]{3,2,1,0:T(8,128)} %up_hbm.1, bf16[768,256]{1,0:T(8,128)(2,1)} %bitcast.5, s32[1,384]{1,0:T(1,128)} %bitcast.6, s32[1,384]{1,0:T(1,128)} %bitcast.7, f32[3,16,16]{2,1,0:T(8,128)} %cpl_hbm.1, ...), custom_call_target="tpu_custom_call" | custom-call | tf_op jit(solution)/shard_map/domain_reduction/pallas_call | solution.py:357
  39.0 0.7 %copy.14 = f32[3,16,16,128]{3,2,1,0:T(8,128)} copy(f32[3,16,16,128]{3,2,1,0:T(8,128)S(1)} %get-tuple-element.2) | data formatting | bytes 786432
  39.7 0.7 %copy.15 = f32[3,16,16,128]{3,2,1,0:T(8,128)} copy(f32[3,16,16,128]{3,2,1,0:T(8,128)S(1)} %get-tuple-element.3) | data formatting | bytes 786432

commit v4 on v3

v4 whole, which is shorter than its diff:
```python
import functools

import jax
import jax.numpy as jnp
import ml_dtypes
import numpy as np
from jax import lax
from jax.experimental import pallas as pl
from jax.experimental.pallas import tpu as pltpu
from jax.sharding import PartitionSpec as P

NSTEP = 4
MESH = pl.DeviceIdType.MESH
F32 = jnp.float32
BF16 = jnp.bfloat16


def wave_table(count):
    half = count // 2
    freq = np.float32(2.0 * np.pi) * (np.arange(half, dtype=np.float32) + np.float32(0.5)) / np.float32(count)
    times = np.float32(37.0) + np.arange(NSTEP, dtype=np.float32)
    phase = (freq[:, None] * times[None, :]).astype(np.float32)
    table = np.concatenate([np.cos(phase), np.sin(phase)], axis=0) / np.sqrt(np.float32(half))
    table = np.pad(table.T, ((0, 8 - NSTEP), (0, 0)))
    return table.astype(ml_dtypes.bfloat16)


def two_parts(b):
    hi = b.astype(BF16)
    lo = (b - hi.astype(F32)).astype(BF16)
    return jnp.concatenate([hi, lo], axis=0)


def kernel(
    n_gx, n_gy, u_hbm, up_hbm, pan_hbm, own_hbm, blk_hbm, cpl_hbm, dep_hbm, spd_hbm, lat_hbm, tab_hbm,
    out_now, out_prev,
    U, up, pan, own, blk, cpl, dep, spd, lat, tab, G, D, msend, mrecv,
    rate, D1, D1x, zsend, zrecv, zside, zrow, in_sem, fsend_sem, frecv_sem, send_sem, recv_sem,
):
    gx, gy, gz = lax.axis_index("gx"), lax.axis_index("gy"), lax.axis_index("gz")
    loads = [
        pltpu.make_async_copy(pan_hbm, pan, in_sem.at[0]),
        pltpu.make_async_copy(tab_hbm, tab, in_sem.at[1]),
        pltpu.make_async_copy(own_hbm, own, in_sem.at[2]),
        pltpu.make_async_copy(blk_hbm, blk, in_sem.at[3]),
        pltpu.make_async_copy(cpl_hbm, cpl, in_sem.at[4]),
        pltpu.make_async_copy(u_hbm, U.at[0, :, 2:18, 16:32], in_sem.at[5]),
        pltpu.make_async_copy(up_hbm, up, in_sem.at[6]),
        pltpu.make_async_copy(lat_hbm, lat.at[1:17, 16:32], in_sem.at[7]),
        pltpu.make_async_copy(dep_hbm, dep, in_sem.at[8]),
        pltpu.make_async_copy(spd_hbm, spd, in_sem.at[9]),
    ]
    for at in (2, 0, 1, 3, 4, 5, 6, 7, 8, 9):
        loads[at].start()

    barrier = pltpu.get_barrier_semaphore()

    has_left, has_right = gx > 0, gx < n_gx - 1
    has_down, has_up = gy > 0, gy < n_gy - 1

    def exists(dx, dy):
        there = gx >= 0
        if dx:
            there = has_right if dx > 0 else has_left
        if dy:
            there = jnp.logical_and(there, has_up if dy > 0 else has_down)
        return there

    def device(dx, dy, dz):
        return {"gx": gx + dx, "gy": gy + dy, "gz": 1 - gz if dz else gz}

    near = [
        (dx, dy, 0) for dx in (-1, 0, 1) for dy in (-1, 0, 1) if dx or dy
    ] + [(0, 0, 1), (-1, 0, 1), (1, 0, 1), (0, -1, 1), (0, 1, 1)]
    count = gy
    for dx, dy, dz in near:
        if (dx, dy, dz) != (0, 1, 0):
            pl.when(exists(dx, dy))(
                lambda to=(dx, dy, dz): pl.semaphore_signal(
                    barrier, inc=1, device_id=device(*to), device_id_type=MESH
                )
            )
        if (dx, dy, dz) != (0, -1, 0):
            count = count + exists(dx, dy).astype(jnp.int32)

    @pl.loop(gy + 1, n_gy)
    def _(peer):
        pl.semaphore_signal(barrier, inc=1, device_id={"gy": peer}, device_id_type=MESH)

    @pl.when(jnp.logical_not(has_left))
    def _():
        U[:, :, 0:2, 8:40] = jnp.zeros((NSTEP, 3, 2, 32, 128), F32)
        lat[0, 16:32] = jnp.zeros((16, 128), F32)
        D1x[0] = jnp.zeros((16, 384), F32)
        zside[0] = jnp.zeros((16, 128), F32)

    @pl.when(jnp.logical_not(has_right))
    def _():
        U[:, :, 18:20, 8:40] = jnp.zeros((NSTEP, 3, 2, 32, 128), F32)
        lat[17, 16:32] = jnp.zeros((16, 128), F32)
        D1x[1] = jnp.zeros((16, 384), F32)
        zside[1] = jnp.zeros((16, 128), F32)

    @pl.when(jnp.logical_not(has_down))
    def _():
        U[:, :, :, 8:16] = jnp.zeros((NSTEP, 3, 20, 8, 128), F32)
        lat[1:17, 8:16] = jnp.zeros((16, 8, 128), F32)
        D1[:, 8:16] = jnp.zeros((16, 8, 384), F32)
        zrow[0] = jnp.zeros((8, 128), F32)

    @pl.when(jnp.logical_not(has_up))
    def _():
        U[:, :, :, 32:40] = jnp.zeros((NSTEP, 3, 20, 8, 128), F32)
        lat[1:17, 32:40] = jnp.zeros((16, 8, 128), F32)
        D1[:, 32:40] = jnp.zeros((16, 8, 384), F32)
        zrow[1] = jnp.zeros((8, 128), F32)

    edge = 127 - 127 * gz
    lane16 = lax.broadcasted_iota(jnp.int32, (16, 128), 1)

    loads[2].wait()
    owner = own[...]
    q = lax.broadcasted_iota(jnp.int32, (1, 384), 1)
    rank = jnp.zeros((1, 384), jnp.int32)
    for d in range(1, 16):
        same = jnp.logical_and(q % 16 >= d, pltpu.roll(owner, d, 1) == owner)
        rank = rank + same.astype(jnp.int32)
    own[...] = owner + 64 * rank

    tile = gy // 8
    off = (gy - 8 * tile) * 16
    lane1 = lax.broadcasted_iota(jnp.int32, (1, 128), 1)
    mycode = own[:, pl.ds(pl.multiple_of(tile * 128, 128), 128)]
    mycode = jnp.where(jnp.logical_and(lane1 >= off, lane1 < off + 16), mycode, 0)
    for s in (16, 32, 64):
        mycode = mycode + pltpu.roll(mycode, s, 1)
    r192 = lax.broadcasted_iota(jnp.int32, (192, 128), 0)
    l192 = lax.broadcasted_iota(jnp.int32, (192, 128), 1)
    want = (r192 % 24) + 64 * (r192 // 96)
    step_of = (r192 // 24) % 4
    pick = jnp.where(jnp.logical_and(mycode == want, l192 // 16 == step_of), 1.0, 0.0).astype(BF16)
    pick = jnp.concatenate([pick, pick], axis=1)

    G[...] = jnp.zeros_like(G)
    loads[4].wait()
    zero = jnp.zeros((16, 16), F32)
    stiff = jnp.concatenate(
        [jnp.concatenate([cpl[c] if c == k else zero for k in range(3)], axis=1) for c in range(3)], axis=0
    )
    loads[0].wait()
    loads[1].wait()
    free = lax.dot_general(tab[...], pan[...], (((1,), (1,)), ((), ())), preferred_element_type=F32)
    for p in range(16):
        G[:, p, :48] = free[:, 48 * p : 48 * p + 48]
    force = lax.dot_general(
        G[...].reshape(128, 128)[:, :48], stiff, (((1,), (1,)), ((), ())),
        precision=lax.Precision.HIGHEST, preferred_element_type=F32,
    )
    picked = jnp.dot(pick, two_parts(force), preferred_element_type=F32)
    picked = jnp.concatenate([picked, jnp.zeros((192, 80), F32)], axis=1)
    lane24 = lax.broadcasted_iota(jnp.int32, (24, 128), 1)
    for c in range(3):
        message = jnp.zeros((24, 128), F32)
        for sn in range(8):
            part = picked[24 * sn : 24 * sn + 24]
            shift = (16 * (sn - c)) % 128
            if shift:
                part = pltpu.roll(part, shift, 1)
            message = jnp.where(lane24 // 16 == sn, part, message)
        msend[:, c, :] = message
    mrecv[gy] = msend[gy]

    loads[5].wait()
    loads[7].wait()
    pl.semaphore_wait(barrier, count)

    def message_copy(peer, sender):
        return pltpu.make_async_remote_copy(
            src_ref=msend.at[peer], dst_ref=mrecv.at[sender], send_sem=fsend_sem.at[peer],
            recv_sem=frecv_sem.at[sender], device_id={"gy": peer}, device_id_type=MESH,
        )

    def exchange(first, moves):
        return [
            (
                to,
                pltpu.make_async_remote_copy(
                    src_ref=src, dst_ref=dst, send_sem=send_sem.at[first + k], recv_sem=recv_sem.at[first + k],
                    device_id=device(*to), device_id_type=MESH,
                ),
            )
            for k, (to, src, dst) in enumerate(moves)
        ]

    def start(copies):
        for to, copy in copies:
            pl.when(exists(to[0], to[1]))(copy.start)

    def arrive(copies):
        for to, copy in copies:
            pl.when(exists(-to[0], -to[1]))(copy.wait_recv)

    def sent(copies):
        for to, copy in copies:
            pl.when(exists(to[0], to[1]))(copy.wait_send)

    def x_faces(step, width):
        return [
            ((-1, 0, 0), U.at[step, :, 2 : 2 + width, 16:32], U.at[step, :, 18 : 18 + width, 16:32]),
            ((1, 0, 0), U.at[step, :, 18 - width : 18, 16:32], U.at[step, :, 2 - width : 2, 16:32]),
        ]

    def y_faces(step, width):
        return [
            ((0, -1, 0), U.at[step, :, 2:18, 16 : 16 + width], U.at[step, :, 2:18, 32 : 32 + width]),
            ((0, 1, 0), U.at[step, :, 2:18, 32 - width : 32], U.at[step, :, 2:18, 16 - width : 16]),
        ]

    first_x = exchange(0, x_faces(0, 1))
    first_yz = exchange(2, y_faces(0, 1) + [
        ((0, 0, 1), zsend.at[0:2], zrecv.at[0:2]),
        ((-1, 0, 0), lat.at[1, 16:32], lat.at[17, 16:32]),
        ((1, 0, 0), lat.at[16, 16:32], lat.at[0, 16:32]),
        ((0, -1, 0), lat.at[1:17, 16:17], lat.at[1:17, 32:33]),
        ((0, 1, 0), lat.at[1:17, 31:32], lat.at[1:17, 15:16]),
    ])
    deep_x = exchange(9, x_faces(1, 2) + [
        ((-1, 0, 0), D1.at[0, 16:32], D1x.at[1]),
        ((1, 0, 0), D1.at[15, 16:32], D1x.at[0]),
    ])
    deep_y = exchange(13, [
        ((dx, dy, 0), U.at[1, :, 2 if dx < 0 else 17, pl.ds(16 if dy < 0 else 31, 1)],
         U.at[1, :, 18 if dx < 0 else 1, pl.ds(32 if dy < 0 else 15, 1)])
        for dx in (-1, 1) for dy in (-1, 1)
    ] + y_faces(1, 2) + [
        ((0, -1, 0), D1.at[:, 16:17], D1.at[:, 32:33]),
        ((0, 1, 0), D1.at[:, 31:32], D1.at[:, 15:16]),
    ])
    deep_z = exchange(21, [
        ((-1, 0, 1), zsend.at[2], zside.at[1]),
        ((1, 0, 1), zsend.at[2], zside.at[0]),
        ((0, -1, 1), zsend.at[2, 0:8], zrow.at[1]),
        ((0, 1, 1), zsend.at[2, 8:16], zrow.at[0]),
        ((0, 0, 1), zsend.at[2:5], zrecv.at[2:5]),
    ])
    last_x = exchange(26, x_faces(3, 1))
    last_yz = exchange(28, y_faces(3, 1) + [((0, 0, 1), zsend.at[5], zrecv.at[5])])

    def pack(place, value, packed):
        turned = pltpu.roll(value, place, 1) if place else value
        return jnp.where(lane16 == jnp.bitwise_and(edge + place, 127), turned, packed)

    start(first_x)

    @pl.loop(0, gy)
    def _(peer):
        message_copy(peer, gy).start()

    for copy in (loads[8], loads[9]):
        copy.wait()
    speed = jnp.zeros((1, 128), F32)
    for layer in range(spd.shape[1]):
        speed = jnp.where(dep[...] == layer, spd[0:1, layer : layer + 1], speed)
    rate[1:17, 16:32] = lat[1:17, 16:32] * speed[None]
    packed, packed_rate = jnp.zeros((16, 128), F32), jnp.zeros((16, 128), F32)
    for c in range(3):
        for x in range(16):
            packed = pack(16 * c + x, U[0, c, x + 2, 16:32], packed)
            packed_rate = pack(16 * c + x, rate[x + 1, 16:32], packed_rate)
    zsend[0] = packed
    zsend[1] = packed_rate
    start(first_yz)

    loads[3].wait()
    k48 = lax.broadcasted_iota(jnp.int32, (48, 384), 0)
    q48 = lax.broadcasted_iota(jnp.int32, (48, 384), 1)
    late = k48 >= 32
    slot = jnp.where(late, (k48 - 32) // 8, k48 // 16)
    src = jnp.where(late, 16 + k48 % 8, k48 % 16)
    mine = jnp.logical_and(own[...] == gy + 64 * slot, q48 // 16 == src)
    slot_block = jnp.sum(jnp.where(mine, blk[...] + 1, 0), axis=1, keepdims=True) - 1
    column = lax.shift_right_arithmetic(slot_block, 3)
    hot = jnp.where(column == lax.broadcasted_iota(jnp.int32, (48, 256), 1), 1.0, 0.0)
    hot = jnp.transpose(jnp.concatenate([hot, jnp.zeros((80, 256), F32)], axis=0)).astype(BF16)
    hot_early = jnp.concatenate([hot[:, :32], hot[:, :32]], axis=1)
    hot_late = jnp.concatenate([hot[:, 32:48], hot[:, 32:48]], axis=1)

    loads[6].wait()

    def turned_rows(first, count, at):
        out = []
        for s in range(2):
            zb = jnp.bitwise_and(slot_block[at + count * s : at + count * (s + 1)], 7)
            for c in range(3):
                row = mrecv[first : first + count, c, :]
                for b in range(3):
                    row = jnp.where(jnp.bitwise_and(zb, 1 << b) > 0, pltpu.roll(row, 16 << b, 1), row)
                out.append((s, c, zb, row))
        return out

    def placed(rows, count, hot, n):
        lanes = lax.broadcasted_iota(jnp.int32, (count, 128), 1) // 16
        parts = [[], []]
        for s, c, zb, row in rows:
            shift = (-16 * (4 * s + n)) % 128
            moved = pltpu.roll(row, shift, 1) if shift else row
            parts[s].append(jnp.where(lanes == zb, moved, 0.0))
        w = jnp.concatenate([jnp.concatenate(part, axis=1) for part in parts], axis=0)
        return jnp.dot(hot, two_parts(w), preferred_element_type=F32)

    def stencil(step, c, x, halo, lo=16, rows=16):
        here = pl.ds(lo, rows)
        v = U[step, c, x + 2, here]
        lanes = lax.broadcasted_iota(jnp.int32, (rows, 128), 1)
        z = (
            jnp.where(lanes == 0, 0.0, pltpu.roll(v, 1, 1))
            + jnp.where(lanes == 127, 0.0, pltpu.roll(v, 127, 1))
            + jnp.where(lanes == edge, halo, 0.0)
        )
        y = U[step, c, x + 2, pl.ds(lo - 1, rows)] + U[step, c, x + 2, pl.ds(lo + 1, rows)]
        around = (U[step, c, x + 1, here] + U[step, c, x + 3, here]) + y + z
        old = up[c, x] if step == 0 else U[step - 1, c, x + 2, here]
        return (2.0 * v - old) + rate[x + 1, here] * (around - 6.0 * v)

    def to_edge(packed, place):
        return pltpu.roll(packed, 128 - place, 1) if place else packed

    order = [0, 15, 1, 14] + list(range(2, 14))

    def received(packed):
        return pltpu.roll(packed, jnp.bitwise_and(127 + 2 * gz, 127), 1)

    arrive(first_yz)
    arrive(first_x)
    rate[0:1, 16:32] = lat[0:1, 16:32] * speed[None]
    rate[17:18, 16:32] = lat[17:18, 16:32] * speed[None]
    rate[1:17, 8:16] = lat[1:17, 8:16] * speed[None]
    rate[1:17, 32:40] = lat[1:17, 32:40] * speed[None]
    halo0 = received(zrecv[0])
    for x in order:
        for c in range(3):
            U[1, c, x + 2, 16:32] = stencil(0, c, x, to_edge(halo0, 16 * c + x))

    def message_wait(peer):
        message_copy(peer, peer).wait_recv()

    def message_reply(peer):
        message_copy(peer, peer).wait_recv()
        message_copy(peer, gy).start()

    turn = jnp.where(gy < 16, 16, n_gy)
    pl.loop(gy + 1, turn)(message_reply)
    pl.loop(0, jnp.minimum(gy, 16))(message_wait)
    rows = turned_rows(0, 16, 0)
    D[0] = placed(rows, 16, hot_early, 0)
    D1[:, 16:32] = placed(rows, 16, hot_early, 1).reshape(16, 16, 384)
    for n in (2, 3):
        D[n - 1] = placed(rows, 16, hot_early, n)
    pl.loop(turn, n_gy)(message_reply)
    pl.loop(16, gy)(message_wait)
    rows = turned_rows(16, 8, 32)
    drive = D[0] + placed(rows, 8, hot_late, 0)
    D1[:, 16:32] = D1[:, 16:32] + placed(rows, 8, hot_late, 1).reshape(16, 16, 384)
    edge_1 = inner_1 = edge_d = jnp.zeros((16, 128), F32)
    inward = jnp.where(gz == 0, 1, 127)
    for x in order:
        for c in range(3):
            new = U[1, c, x + 2, 16:32] + drive[16 * x : 16 * x + 16, 128 * c : 128 * c + 128]
            U[1, c, x + 2, 16:32] = new
            edge_1 = pack(16 * c + x, new, edge_1)
            inner_1 = pack(16 * c + x, pltpu.roll(new, inward, 1), inner_1)
            edge_d = pack(16 * c + x, D1[x, 16:32, 128 * c : 128 * c + 128], edge_d)
        if x == 14:
            start(deep_x)
    zsend[2] = edge_1
    zsend[3] = inner_1
    zsend[4] = edge_d
    start(deep_y)
    start(deep_z)
    for n in (2, 3):
        D[n - 1] = D[n - 1] + placed(rows, 8, hot_late, n)

    arrive(deep_z)
    arrive(deep_y)
    arrive(deep_x)
    halo1 = received(zrecv[2])
    left1, right1 = received(zside[0]), received(zside[1])
    tall = received(jnp.concatenate([zrow[0], zrecv[2], zrow[1]], axis=0))[4:28]
    for c in range(3):
        U[2, c, 1, 16:32] = stencil(1, c, -1, to_edge(left1, 16 * c + 15)) + D1x[0, :, 128 * c : 128 * c + 128]
        U[2, c, 18, 16:32] = stencil(1, c, 16, to_edge(right1, 16 * c)) + D1x[1, :, 128 * c : 128 * c + 128]
        for x in range(16):
            U[2, c, x + 2, 12:36] = (
                stencil(1, c, x, to_edge(tall, 16 * c + x), 12, 24) + D1[x, 12:36, 128 * c : 128 * c + 128]
            )
    x_of = jnp.bitwise_and(lane16 - edge, 15)
    row16 = lax.broadcasted_iota(jnp.int32, (16, 128), 0)
    beside = (
        jnp.where(x_of == 0, pltpu.roll(left1, 113, 1), pltpu.roll(halo1, 1, 1))
        + jnp.where(x_of == 15, pltpu.roll(right1, 15, 1), pltpu.roll(halo1, 127, 1))
        + tall[3:19] + tall[5:21] + edge_1 + received(zrecv[3])
    )
    halo = (2.0 * halo1 - halo0) + received(zrecv[1]) * (beside - 6.0 * halo1) + received(zrecv[4])

    packed = jnp.zeros((16, 128), F32)
    for x in order:
        for c in range(3):
            drive = D[1, 16 * x : 16 * x + 16, 128 * c : 128 * c + 128]
            new = stencil(2, c, x, to_edge(halo, 16 * c + x)) + drive
            U[3, c, x + 2, 16:32] = new
            packed = pack(16 * c + x, new, packed)
            out_prev[c, x] = new
        if x == 15:
            start(last_x)
    zsend[5] = packed
    start(last_yz)

    arrive(last_yz)
    arrive(last_x)
    halo = received(zrecv[5])
    for x in order:
        for c in range(3):
            drive = D[2, 16 * x : 16 * x + 16, 128 * c : 128 * c + 128]
            out_now[c, x] = stencil(3, c, x, to_edge(halo, 16 * c + x)) + drive

    for copies in (first_x, first_yz, deep_x, deep_y, deep_z, last_x, last_yz):
        sent(copies)

    @pl.loop(1, n_gy)
    def _(k):
        message_copy(lax.rem(gy + k, n_gy), gy).wait_send()


def per_device(n_gx, n_gy, u_now, u_prev, panels, panel_owner, panel_block, coupling, layer_depth, layer_speed, lateral):
    spectral = panels.shape[4]
    count = panel_owner.shape[2]
    layers = layer_speed.shape[0]
    table = jnp.asarray(wave_table(spectral))
    anywhere = pl.BlockSpec(memory_space=pl.ANY)
    vmem = pl.BlockSpec(memory_space=pltpu.VMEM)
    dma = pltpu.SemaphoreType.DMA
    return pl.pallas_call(
        functools.partial(kernel, n_gx, n_gy),
        out_shape=(pltpu.VMEM(u_now.shape, F32), pltpu.VMEM(u_now.shape, F32)),
        in_specs=[anywhere] * 10,
        out_specs=(vmem, vmem),
        scratch_shapes=[
            pltpu.VMEM((NSTEP, 3, 20, 48, 128), F32),
            pltpu.VMEM(u_prev.shape, F32),
            pltpu.VMEM((768, spectral), BF16),
            pltpu.VMEM((1, count), jnp.int32),
            pltpu.VMEM((1, count), jnp.int32),
            pltpu.VMEM(coupling.shape, F32),
            pltpu.VMEM((1, 128), jnp.int32),
            pltpu.VMEM((1, layers), F32),
            pltpu.VMEM((18, 48, 128), F32),
            pltpu.VMEM(table.shape, BF16),
            pltpu.VMEM((8, 16, 128), F32),
            pltpu.VMEM((3, 256, 384), F32),
            pltpu.VMEM((24, 3, 128), F32),
            pltpu.VMEM((24, 3, 128), F32),
            pltpu.VMEM((18, 48, 128), F32),
            pltpu.VMEM((16, 48, 384), F32),
            pltpu.VMEM((2, 16, 384), F32),
            pltpu.VMEM((6, 16, 128), F32),
            pltpu.VMEM((6, 16, 128), F32),
            pltpu.VMEM((2, 16, 128), F32),
            pltpu.VMEM((2, 8, 128), F32),
            dma((10,)),
            dma((24,)),
            dma((24,)),
            dma((31,)),
            dma((31,)),
        ],
        compiler_params=pltpu.CompilerParams(collective_id=0, has_side_effects=True),
        name="domain_reduction",
    )(
        u_now, u_prev, panels.reshape(768, spectral), panel_owner.reshape(1, count), panel_block.reshape(1, count),
        coupling, layer_depth.reshape(1, 128), layer_speed.reshape(1, layers), lateral, table,
    )


def solution(mesh):
    in_specs = (
        P(None, "gx", "gy", "gz"),
        P(None, "gx", "gy", "gz"),
        P("gx", "gz", "gy", None, None),
        P("gx", "gz", None, None),
        P("gx", "gz", None),
        P(),
        P("gz"),
        P(),
        P("gx", "gy", "gz"),
    )
    out_specs = (P(None, "gx", "gy", "gz"), P(None, "gx", "gy", "gz"))
    return jax.shard_map(
        functools.partial(per_device, mesh.shape["gx"], mesh.shape["gy"]),
        mesh=mesh, in_specs=in_specs, out_specs=out_specs, check_vma=False,
    )
```

time: 40.6 us -> 37.5 us (0.924)
  the two profiles are of different devices: /device:TPU:647 before, /device:TPU:1 now
where the time goes in v4:
time: 37.5 us; the launch traced here: 36.9 us
  Pallas kernels  34.8 us (93%)
  local copies, waits for them, and re-layouts  1.49 us (4%)
  between operations  0.64 us (2%)
    pallas_call x1, Pallas kernels, per_device(): pl.pallas_call(functools.partial(kernel, n_gx, n_gy), out_shape=(pltpu.VM...  34.8 us
    unnamed x2, local copies, waits for them, and re-layouts  1.49 us

profile of v4, /device:TPU:1, one launch (start us, length us, event | category | flops | bytes accessed | tf_op | source)
XLA Modules:
  0.0 36.9 jit_solution(14587041661267506070)
XLA Ops:
  0.6 34.8 %domain_reduction.1 = (f32[3,16,16,128]{3,2,1,0:T(8,128)S(1)}, f32[3,16,16,128]{3,2,1,0:T(8,128)S(1)}) custom-call(f32[3,16,16,128]{3,2,1,0:T(8,128)} %u_hbm.1, f32[3,16,16,128]{3,2,1,0:T(8,128)} %up_hbm.1, bf16[768,256]{1,0:T(8,128)(2,1)} %bitcast.5, s32[1,384]{1,0:T(1,128)} %bitcast.6, s32[1,384]{1,0:T(1,128)} %bitcast.7, f32[3,16,16]{2,1,0:T(8,128)} %cpl_hbm.1, ...), custom_call_target="tpu_custom_call" | custom-call | tf_op jit(solution)/shard_map/domain_reduction/pallas_call | solution.py:442
  35.4 0.7 %copy.14 = f32[3,16,16,128]{3,2,1,0:T(8,128)} copy(f32[3,16,16,128]{3,2,1,0:T(8,128)S(1)} %get-tuple-element.2) | data formatting | bytes 786432
  36.1 0.7 %copy.15 = f32[3,16,16,128]{3,2,1,0:T(8,128)} copy(f32[3,16,16,128]{3,2,1,0:T(8,128)S(1)} %get-tuple-element.3) | data formatting | bytes 786432

commit v5 on v4

--- a/solution.py
+++ b/solution.py
@@ -35,7 +35,7 @@
     n_gx, n_gy, u_hbm, up_hbm, pan_hbm, own_hbm, blk_hbm, cpl_hbm, dep_hbm, spd_hbm, lat_hbm, tab_hbm,
     out_now, out_prev,
     U, up, pan, own, blk, cpl, dep, spd, lat, tab, G, D, msend, mrecv,
-    rate, D1, D1x, zsend, zrecv, zside, zrow, in_sem, fsend_sem, frecv_sem, send_sem, recv_sem,
+    rate, D1, D1x, zsend, zrecv, zside, zrow, in_sem, fsend_sem, frecv_sem, send_sem, recv_sem, known,
 ):
     gx, gy, gz = lax.axis_index("gx"), lax.axis_index("gy"), lax.axis_index("gz")
     loads = [
@@ -69,19 +69,23 @@
     def device(dx, dy, dz):
         return {"gx": gx + dx, "gy": gy + dy, "gz": 1 - gz if dz else gz}
 
-    near = [
-        (dx, dy, 0) for dx in (-1, 0, 1) for dy in (-1, 0, 1) if dx or dy
-    ] + [(0, 0, 1), (-1, 0, 1), (1, 0, 1), (0, -1, 1), (0, 1, 1)]
-    count = gy
-    for dx, dy, dz in near:
-        if (dx, dy, dz) != (0, 1, 0):
-            pl.when(exists(dx, dy))(
-                lambda to=(dx, dy, dz): pl.semaphore_signal(
-                    barrier, inc=1, device_id=device(*to), device_id_type=MESH
-                )
-            )
-        if (dx, dy, dz) != (0, -1, 0):
-            count = count + exists(dx, dy).astype(jnp.int32)
+    middle = n_gx // 2
+    lead_left = jnp.logical_and(has_left, gx != middle)
+    lead_right = gx == middle - 1
+    lead_z = gz == 1
+    told_right = jnp.logical_and(has_right, gx != middle - 1)
+
+    def tell(there, to):
+        pl.when(there)(
+            lambda: pl.semaphore_signal(barrier, inc=1, device_id=device(*to), device_id_type=MESH)
+        )
+
+    tell(gx == middle, (-1, 0, 0))
+    tell(told_right, (1, 0, 0))
+    lonely = jnp.logical_and(gy == 0, jnp.logical_or(gx == 0, gx == middle))
+    tell(jnp.logical_or(gz == 0, lonely), (0, 0, 1))
+    told_z = jnp.logical_or(lead_z, lonely)
+    count = gy + lead_left.astype(jnp.int32) + lead_right.astype(jnp.int32) + told_z.astype(jnp.int32)
 
     @pl.loop(gy + 1, n_gy)
     def _(peer):
@@ -216,14 +220,12 @@
             ((0, 1, 0), U.at[step, :, 2:18, 32 - width : 32], U.at[step, :, 2:18, 16 - width : 16]),
         ]
 
-    first_x = exchange(0, x_faces(0, 1))
-    first_yz = exchange(2, y_faces(0, 1) + [
-        ((0, 0, 1), zsend.at[0:2], zrecv.at[0:2]),
-        ((-1, 0, 0), lat.at[1, 16:32], lat.at[17, 16:32]),
-        ((1, 0, 0), lat.at[16, 16:32], lat.at[0, 16:32]),
-        ((0, -1, 0), lat.at[1:17, 16:17], lat.at[1:17, 32:33]),
-        ((0, 1, 0), lat.at[1:17, 31:32], lat.at[1:17, 15:16]),
-    ])
+    (u_left, u_right), (u_down, u_up) = x_faces(0, 1), y_faces(0, 1)
+    left = exchange(0, [u_left, ((-1, 0, 0), lat.at[1, 16:32], lat.at[17, 16:32])])
+    right = exchange(2, [u_right, ((1, 0, 0), lat.at[16, 16:32], lat.at[0, 16:32])])
+    down = exchange(4, [u_down, ((0, -1, 0), lat.at[1:17, 16:17], lat.at[1:17, 32:33])])
+    up_gy = exchange(6, [u_up, ((0, 1, 0), lat.at[1:17, 31:32], lat.at[1:17, 15:16])])
+    across = exchange(8, [((0, 0, 1), zsend.at[0:2], zrecv.at[0:2])])
     deep_x = exchange(9, x_faces(1, 2) + [
         ((-1, 0, 0), D1.at[0, 16:32], D1x.at[1]),
         ((1, 0, 0), D1.at[15, 16:32], D1x.at[0]),
@@ -250,11 +252,13 @@
         turned = pltpu.roll(value, place, 1) if place else value
         return jnp.where(lane16 == jnp.bitwise_and(edge + place, 127), turned, packed)
 
-    start(first_x)
-
     @pl.loop(0, gy)
     def _(peer):
         message_copy(peer, gy).start()
+
+    pl.when(lead_left)(lambda: start(left))
+    pl.when(lead_right)(lambda: start(right))
+    start(down)
 
     for copy in (loads[8], loads[9]):
         copy.wait()
@@ -269,7 +273,7 @@
             packed_rate = pack(16 * c + x, rate[x + 1, 16:32], packed_rate)
     zsend[0] = packed
     zsend[1] = packed_rate
-    start(first_yz)
+    pl.when(lead_z)(lambda: start(across))
 
     loads[3].wait()
     k48 = lax.broadcasted_iota(jnp.int32, (48, 384), 0)
@@ -330,8 +334,36 @@
     def received(packed):
         return pltpu.roll(packed, jnp.bitwise_and(127 + 2 * gz, 127), 1)
 
-    arrive(first_yz)
-    arrive(first_x)
+    def answer(came, reply):
+        arrive(came)
+        start(reply)
+
+    pl.when(jnp.logical_not(lead_z))(lambda: answer(across, across))
+    answer(down, up_gy)
+    pl.when(jnp.logical_not(lead_right))(lambda: answer(left, right))
+    pl.when(gx == middle)(lambda: answer(right, left))
+
+    def message_wait(peer):
+        message_copy(peer, peer).wait_recv()
+
+    def message_reply(peer):
+        message_copy(peer, peer).wait_recv()
+        message_copy(peer, gy).start()
+
+    answered = jnp.where(jnp.logical_and(gx == 0, gy == 0), 16, gy + 1)
+    pl.loop(gy + 1, answered)(message_reply)
+    pl.when(lead_z)(lambda: arrive(across))
+    arrive(up_gy)
+    pl.when(lead_right)(lambda: arrive(left))
+    pl.when(gx != middle)(lambda: arrive(right))
+    sides = [(-1, 0, 0), (1, 0, 0), (0, -1, 0), (0, 1, 0)]
+    beside_count = 0
+    for to in sides:
+        there = exists(to[0], to[1])
+        beside_count = beside_count + there.astype(jnp.int32)
+        pl.when(there)(
+            lambda to=to: pl.semaphore_signal(known, inc=1, device_id=device(*to), device_id_type=MESH)
+        )
     rate[0:1, 16:32] = lat[0:1, 16:32] * speed[None]
     rate[17:18, 16:32] = lat[17:18, 16:32] * speed[None]
     rate[1:17, 8:16] = lat[1:17, 8:16] * speed[None]
@@ -341,15 +373,8 @@
         for c in range(3):
             U[1, c, x + 2, 16:32] = stencil(0, c, x, to_edge(halo0, 16 * c + x))
 
-    def message_wait(peer):
-        message_copy(peer, peer).wait_recv()
-
-    def message_reply(peer):
-        message_copy(peer, peer).wait_recv()
-        message_copy(peer, gy).start()
-
-    turn = jnp.where(gy < 16, 16, n_gy)
-    pl.loop(gy + 1, turn)(message_reply)
+    turn = jnp.where(gy < 8, 16, n_gy)
+    pl.loop(answered, turn)(message_reply)
     pl.loop(0, jnp.minimum(gy, 16))(message_wait)
     rows = turned_rows(0, 16, 0)
     D[0] = placed(rows, 16, hot_early, 0)
@@ -375,6 +400,7 @@
     zsend[2] = edge_1
     zsend[3] = inner_1
     zsend[4] = edge_d
+    pl.semaphore_wait(known, beside_count)
     start(deep_y)
     start(deep_z)
     for n in (2, 3):
@@ -423,7 +449,7 @@
             drive = D[2, 16 * x : 16 * x + 16, 128 * c : 128 * c + 128]
             out_now[c, x] = stencil(3, c, x, to_edge(halo, 16 * c + x)) + drive
 
-    for copies in (first_x, first_yz, deep_x, deep_y, deep_z, last_x, last_yz):
+    for copies in (left, right, down, up_gy, across, deep_x, deep_y, deep_z, last_x, last_yz):
         sent(copies)
 
     @pl.loop(1, n_gy)
@@ -471,6 +497,7 @@
             dma((24,)),
             dma((31,)),
             dma((31,)),
+            pltpu.SemaphoreType.REGULAR,
         ],
         compiler_params=pltpu.CompilerParams(collective_id=0, has_side_effects=True),
         name="domain_reduction",

time: 37.5 us -> 36.9 us (0.984); the launches traced: 36.9 us -> 36.7 us
  no operation moved by 1% of the time
where the time goes in v5:
time: 36.9 us; the launch traced here: 36.7 us
  Pallas kernels  34.6 us (94%)
  local copies, waits for them, and re-layouts  1.49 us (4%)
  between operations  0.64 us (2%)
    pallas_call x1, Pallas kernels, per_device(): pl.pallas_call(functools.partial(kernel, n_gx, n_gy), out_shape=(pltpu.VM...  34.6 us
    unnamed x2, local copies, waits for them, and re-layouts  1.49 us

profile of v5, /device:TPU:1, one launch (start us, length us, event | category | flops | bytes accessed | tf_op | source)
XLA Modules:
  0.0 36.7 jit_solution(8106466354650099345)
XLA Ops:
  0.6 34.6 %domain_reduction.1 = (f32[3,16,16,128]{3,2,1,0:T(8,128)S(1)}, f32[3,16,16,128]{3,2,1,0:T(8,128)S(1)}) custom-call(f32[3,16,16,128]{3,2,1,0:T(8,128)} %u_hbm.1, f32[3,16,16,128]{3,2,1,0:T(8,128)} %up_hbm.1, bf16[768,256]{1,0:T(8,128)(2,1)} %bitcast.5, s32[1,384]{1,0:T(1,128)} %bitcast.6, s32[1,384]{1,0:T(1,128)} %bitcast.7, f32[3,16,16]{2,1,0:T(8,128)} %cpl_hbm.1, ...), custom_call_target="tpu_custom_call" | custom-call | tf_op jit(solution)/shard_map/domain_reduction/pallas_call | solution.py:468
  35.3 0.7 %copy.14 = f32[3,16,16,128]{3,2,1,0:T(8,128)} copy(f32[3,16,16,128]{3,2,1,0:T(8,128)S(1)} %get-tuple-element.2) | data formatting | bytes 786432
  36.0 0.7 %copy.15 = f32[3,16,16,128]{3,2,1,0:T(8,128)} copy(f32[3,16,16,128]{3,2,1,0:T(8,128)S(1)} %get-tuple-element.3) | data formatting | bytes 786432

commit v6 on v5

--- a/solution.py
+++ b/solution.py
@@ -230,17 +230,20 @@
         ((-1, 0, 0), D1.at[0, 16:32], D1x.at[1]),
         ((1, 0, 0), D1.at[15, 16:32], D1x.at[0]),
     ])
-    deep_y = exchange(13, [
+    corners = exchange(13, [
         ((dx, dy, 0), U.at[1, :, 2 if dx < 0 else 17, pl.ds(16 if dy < 0 else 31, 1)],
          U.at[1, :, 18 if dx < 0 else 1, pl.ds(32 if dy < 0 else 15, 1)])
         for dx in (-1, 1) for dy in (-1, 1)
-    ] + y_faces(1, 2) + [
+    ])
+    deep_y = exchange(17, y_faces(1, 2) + [
         ((0, -1, 0), D1.at[:, 16:17], D1.at[:, 32:33]),
         ((0, 1, 0), D1.at[:, 31:32], D1.at[:, 15:16]),
     ])
-    deep_z = exchange(21, [
+    deep_xz = exchange(21, [
         ((-1, 0, 1), zsend.at[2], zside.at[1]),
         ((1, 0, 1), zsend.at[2], zside.at[0]),
+    ])
+    deep_z = exchange(23, [
         ((0, -1, 1), zsend.at[2, 0:8], zrow.at[1]),
         ((0, 1, 1), zsend.at[2, 8:16], zrow.at[0]),
         ((0, 0, 1), zsend.at[2:5], zrecv.at[2:5]),
@@ -401,6 +404,8 @@
     zsend[3] = inner_1
     zsend[4] = edge_d
     pl.semaphore_wait(known, beside_count)
+    start(corners)
+    start(deep_xz)
     start(deep_y)
     start(deep_z)
     for n in (2, 3):
@@ -408,19 +413,27 @@
 
     arrive(deep_z)
     arrive(deep_y)
+    halo1 = received(zrecv[2])
+    tall = received(jnp.concatenate([zrow[0], zrecv[2], zrow[1]], axis=0))[4:28]
+
+    def second(x):
+        for c in range(3):
+            U[2, c, x + 2, 12:36] = (
+                stencil(1, c, x, to_edge(tall, 16 * c + x), 12, 24) + D1[x, 12:36, 128 * c : 128 * c + 128]
+            )
+
+    for x in range(1, 15):
+        second(x)
+    arrive(corners)
+    arrive(deep_xz)
     arrive(deep_x)
-    halo1 = received(zrecv[2])
     left1, right1 = received(zside[0]), received(zside[1])
-    tall = received(jnp.concatenate([zrow[0], zrecv[2], zrow[1]], axis=0))[4:28]
     for c in range(3):
         U[2, c, 1, 16:32] = stencil(1, c, -1, to_edge(left1, 16 * c + 15)) + D1x[0, :, 128 * c : 128 * c + 128]
         U[2, c, 18, 16:32] = stencil(1, c, 16, to_edge(right1, 16 * c)) + D1x[1, :, 128 * c : 128 * c + 128]
-        for x in range(16):
-            U[2, c, x + 2, 12:36] = (
-                stencil(1, c, x, to_edge(tall, 16 * c + x), 12, 24) + D1[x, 12:36, 128 * c : 128 * c + 128]
-            )
+    second(0)
+    second(15)
     x_of = jnp.bitwise_and(lane16 - edge, 15)
-    row16 = lax.broadcasted_iota(jnp.int32, (16, 128), 0)
     beside = (
         jnp.where(x_of == 0, pltpu.roll(left1, 113, 1), pltpu.roll(halo1, 1, 1))
         + jnp.where(x_of == 15, pltpu.roll(right1, 15, 1), pltpu.roll(halo1, 127, 1))
@@ -442,19 +455,33 @@
     start(last_yz)
 
     arrive(last_yz)
-    arrive(last_x)
     halo = received(zrecv[5])
-    for x in order:
+
+    def last(x):
         for c in range(3):
             drive = D[2, 16 * x : 16 * x + 16, 128 * c : 128 * c + 128]
             out_now[c, x] = stencil(3, c, x, to_edge(halo, 16 * c + x)) + drive
 
-    for copies in (left, right, down, up_gy, across, deep_x, deep_y, deep_z, last_x, last_yz):
+    for x in range(1, 15):
+        last(x)
+    arrive(last_x)
+    last(0)
+    last(15)
+
+    for copies in (left, right, down, up_gy, across, deep_x, corners, deep_y, deep_xz, deep_z, last_x, last_yz):
         sent(copies)
 
     @pl.loop(1, n_gy)
     def _(k):
         message_copy(lax.rem(gy + k, n_gy), gy).wait_send()
+
+
+def write_out(now_in, prev_in, now_out, prev_out, sem):
+    copies = [pltpu.make_async_copy(now_in, now_out, sem.at[0]), pltpu.make_async_copy(prev_in, prev_out, sem.at[1])]
+    for copy in copies:
+        copy.start()
+    for copy in copies:
+        copy.wait()
 
 
 def per_device(n_gx, n_gy, u_now, u_prev, panels, panel_owner, panel_block, coupling, layer_depth, layer_speed, lateral):
@@ -465,7 +492,7 @@
     anywhere = pl.BlockSpec(memory_space=pl.ANY)
     vmem = pl.BlockSpec(memory_space=pltpu.VMEM)
     dma = pltpu.SemaphoreType.DMA
-    return pl.pallas_call(
+    now, prev = pl.pallas_call(
         functools.partial(kernel, n_gx, n_gy),
         out_shape=(pltpu.VMEM(u_now.shape, F32), pltpu.VMEM(u_now.shape, F32)),
         in_specs=[anywhere] * 10,
@@ -505,6 +532,18 @@
         u_now, u_prev, panels.reshape(768, spectral), panel_owner.reshape(1, count), panel_block.reshape(1, count),
         coupling, layer_depth.reshape(1, 128), layer_speed.reshape(1, layers), lateral, table,
     )
+    whole = jax.ShapeDtypeStruct(u_now.shape, F32)
+    return pl.pallas_call(
+        write_out,
+        out_shape=(whole, whole),
+        in_specs=[vmem, vmem],
+        out_specs=(anywhere, anywhere),
+        scratch_shapes=[dma((2,))],
+        name="write_out",
+    )(
+        pltpu.with_memory_space_constraint(now, pltpu.VMEM),
+        pltpu.with_memory_space_constraint(prev, pltpu.VMEM),
+    )
 
 
 def solution(mesh):

time: 36.9 us -> 36.5 us (0.989)
  local copies, waits for them, and re-layouts: 1.49 us -> 0 us
  Pallas kernels: 34.6 us -> 35.7 us
    unnamed x2 -> x0, local copies, waits for them, and re-layouts: 1.49 us -> none
    pallas_call x0 -> x1, Pallas kernels: none -> 0.89 us  [per_device(): pl.pallas_call(write_out, out_shape=(whole, whole), in_specs=[vmem, vmem]...]
where the time goes in v6:
time: 36.5 us; the launch traced here: 36.4 us
  Pallas kernels  35.7 us (98%)
  between operations  0.64 us (2%)
    pallas_call x1, Pallas kernels, per_device(): pl.pallas_call(functools.partial(kernel, n_gx, n_gy), out_shape=(pltpu.VM...  34.8 us
    pallas_call x1, Pallas kernels, per_device(): pl.pallas_call(write_out, out_shape=(whole, whole), in_specs=[vmem, vmem]...  0.89 us

profile of v6, /device:TPU:1, one launch (start us, length us, event | category | flops | bytes accessed | tf_op | source)
XLA Modules:
  0.0 36.4 jit_solution(124853773329866667)
XLA Ops:
  0.6 34.8 %domain_reduction.1 = (f32[3,16,16,128]{3,2,1,0:T(8,128)S(1)}, f32[3,16,16,128]{3,2,1,0:T(8,128)S(1)}) custom-call(f32[3,16,16,128]{3,2,1,0:T(8,128)} %u_hbm.1, f32[3,16,16,128]{3,2,1,0:T(8,128)} %up_hbm.1, bf16[768,256]{1,0:T(8,128)(2,1)} %bitcast.5, s32[1,384]{1,0:T(1,128)} %bitcast.6, s32[1,384]{1,0:T(1,128)} %bitcast.7, f32[3,16,16]{2,1,0:T(8,128)} %cpl_hbm.1, ...), custom_call_target="tpu_custom_call" | custom-call | tf_op jit(solution)/shard_map/domain_reduction/pallas_call | solution.py:495
  35.5 0.9 %write_out.1 = (f32[3,16,16,128]{3,2,1,0:T(8,128)}, f32[3,16,16,128]{3,2,1,0:T(8,128)}) custom-call(f32[3,16,16,128]{3,2,1,0:T(8,128)S(1)} %get-tuple-element.4.now_in, f32[3,16,16,128]{3,2,1,0:T(8,128)S(1)} %get-tuple-element.5.prev_in), custom_call_target="tpu_custom_call" | custom-call | tf_op jit(solution)/shard_map/write_out/pallas_call | solution.py:536

commit v7 on v6

--- a/solution.py
+++ b/solution.py
@@ -305,13 +305,14 @@
                 out.append((s, c, zb, row))
         return out
 
-    def placed(rows, count, hot, n):
+    def placed(rows, count, hot, *steps):
         lanes = lax.broadcasted_iota(jnp.int32, (count, 128), 1) // 16
         parts = [[], []]
-        for s, c, zb, row in rows:
-            shift = (-16 * (4 * s + n)) % 128
-            moved = pltpu.roll(row, shift, 1) if shift else row
-            parts[s].append(jnp.where(lanes == zb, moved, 0.0))
+        for n in steps:
+            for s, c, zb, row in rows:
+                shift = (-16 * (4 * s + n)) % 128
+                moved = pltpu.roll(row, shift, 1) if shift else row
+                parts[s].append(jnp.where(lanes == zb, moved, 0.0))
         w = jnp.concatenate([jnp.concatenate(part, axis=1) for part in parts], axis=0)
         return jnp.dot(hot, two_parts(w), preferred_element_type=F32)
 
@@ -353,7 +354,7 @@
         message_copy(peer, peer).wait_recv()
         message_copy(peer, gy).start()
 
-    answered = jnp.where(jnp.logical_and(gx == 0, gy == 0), 16, gy + 1)
+    answered = jnp.where(jnp.logical_and(gx == 0, gy == 0), 6, gy + 1)
     pl.loop(gy + 1, answered)(message_reply)
     pl.when(lead_z)(lambda: arrive(across))
     arrive(up_gy)
@@ -387,8 +388,9 @@
     pl.loop(turn, n_gy)(message_reply)
     pl.loop(16, gy)(message_wait)
     rows = turned_rows(16, 8, 32)
-    drive = D[0] + placed(rows, 8, hot_late, 0)
-    D1[:, 16:32] = D1[:, 16:32] + placed(rows, 8, hot_late, 1).reshape(16, 16, 384)
+    both = placed(rows, 8, hot_late, 0, 1)
+    drive = D[0] + both[:, :384]
+    D1[:, 16:32] = D1[:, 16:32] + both[:, 384:].reshape(16, 16, 384)
     edge_1 = inner_1 = edge_d = jnp.zeros((16, 128), F32)
     inward = jnp.where(gz == 0, 1, 127)
     for x in order:

time: 36.5 us -> 36.6 us (level)
  no operation moved by 1% of the time
where the time goes in v7:
time: 36.6 us; the launch traced here: 36.5 us
  Pallas kernels  35.8 us (98%)
  between operations  0.64 us (2%)
    pallas_call x1, Pallas kernels, per_device(): pl.pallas_call(functools.partial(kernel, n_gx, n_gy), out_shape=(pltpu.VM...  34.9 us
    pallas_call x1, Pallas kernels, per_device(): pl.pallas_call(write_out, out_shape=(whole, whole), in_specs=[vmem, vmem]...  0.89 us

profile of v7, /device:TPU:1, one launch (start us, length us, event | category | flops | bytes accessed | tf_op | source)
XLA Modules:
  0.0 36.5 jit_solution(5759742599395960343)
XLA Ops:
  0.6 34.9 %domain_reduction.1 = (f32[3,16,16,128]{3,2,1,0:T(8,128)S(1)}, f32[3,16,16,128]{3,2,1,0:T(8,128)S(1)}) custom-call(f32[3,16,16,128]{3,2,1,0:T(8,128)} %u_hbm.1, f32[3,16,16,128]{3,2,1,0:T(8,128)} %up_hbm.1, bf16[768,256]{1,0:T(8,128)(2,1)} %bitcast.5, s32[1,384]{1,0:T(1,128)} %bitcast.6, s32[1,384]{1,0:T(1,128)} %bitcast.7, f32[3,16,16]{2,1,0:T(8,128)} %cpl_hbm.1, ...), custom_call_target="tpu_custom_call" | custom-call | tf_op jit(solution)/shard_map/domain_reduction/pallas_call | solution.py:497
  35.6 0.9 %write_out.1 = (f32[3,16,16,128]{3,2,1,0:T(8,128)}, f32[3,16,16,128]{3,2,1,0:T(8,128)}) custom-call(f32[3,16,16,128]{3,2,1,0:T(8,128)S(1)} %get-tuple-element.4.now_in, f32[3,16,16,128]{3,2,1,0:T(8,128)S(1)} %get-tuple-element.5.prev_in), custom_call_target="tpu_custom_call" | custom-call | tf_op jit(solution)/shard_map/write_out/pallas_call | solution.py:538
